TPU v7x, 256 devices: a whole 4x4x8 slice. The times are simulated.
256 devices in a mesh: dp: 8 (over x, core), space: 32 (over y, z).
Axes of the slice: x: 4, y: 4, z: 8, core: 2. Of those that a mesh axis runs over, the one named last changes fastest.
Arguments:
- features: bfloat16 [8, 262144, 128], P('dp', 'space'), may hold values from -6 to 6
- child_parent: int32 [8, 262144], P('dp', 'space'), may hold values from 0 to 65535, as said below
- child_code: int32 [8, 262144], P('dp', 'space'), may hold values from 0 to 7
- weight: bfloat16 [8, 128, 128], replicated, may hold values from -0.25 to 0.25
- out_grad: bfloat16 [8, 65536, 128], P('dp', 'space'), may hold values from -6 to 6
Outputs:
- parent_out: bfloat16 [8, 65536, 128], P('dp', 'space')
- feature_grad: bfloat16 [8, 262144, 128], P('dp', 'space')
- weight_grad: float32 [8, 128, 128], replicated
Inputs may be any that keep to these rules, and one draw needn't show every extreme that they name: Within one window, child_parent is nondecreasing along the 8192 rows of one device of space. Parent p lies on device p // 2048 of space; at most 512 rows of one device have their parent on one device, and on every device some device receives exactly 512. No two fine octants of a window share both parent and child_code.
All inputs are finite; a program needn't handle non-finite values.
Results may differ from a plain program's by a relative error of at most 0.001.
Values may be sent and summed in bfloat16 or wider, within the bound.
A program may use at most 128 MiB of HBM per device.

v0:
```python
import jax
import jax.numpy as jnp
from jax import lax
from jax.experimental import pallas as pl
from jax.experimental.pallas import tpu as pltpu
from jax.sharding import PartitionSpec as P


MESH = pl.DeviceIdType.MESH
NY = 4
NZ = 8
NS = NY * NZ
ND = 8
CAP = 528
KINDS = 8
PAR = 2048
SLOTS = KINDS * PAR
F32 = jnp.float32
BF16 = jnp.bfloat16
I32 = jnp.int32
ANY = pl.BlockSpec(memory_space=pl.ANY)
VM = pl.BlockSpec(memory_space=pltpu.VMEM)
SM = pl.BlockSpec(memory_space=pltpu.SMEM)
VLIM = 60 * 1024 * 1024


def cost(us):
    return pl.CostEstimate(flops=0, bytes_accessed=int(us * 3.6e6), transcendentals=0)


def pack_kernel(parent_ref, code_ref, feat_ref, blk_ref, slots_ref, rows_ref, first_ref, lo_ref, hi_ref, par, kind):
    step = pl.program_id(0)
    n = feat_ref.shape[0]

    @pl.when(step == 0)
    def _():
        whole = parent_ref[...]
        par[0 : n // 128, :] = whole
        kind[0 : n // 128, :] = code_ref[...]
        begin = jnp.int32(0)
        for d in range(NS):
            below = jnp.sum((whole < (d + 1) * PAR).astype(F32), axis=0, keepdims=True)
            end = jnp.sum(below).astype(I32)
            first = jnp.minimum(begin // 16 * 16, n - CAP)
            first_ref[d] = first
            lo_ref[d] = begin - first
            hi_ref[d] = end - first
            begin = end

    lane = lax.broadcasted_iota(I32, (8, 128), 1)
    pos = lax.broadcasted_iota(I32, (8, 128), 0) * 128 + lane

    def block(b, c):
        d = step * NZ + b
        first = pl.multiple_of(first_ref[d], 16)
        lo, hi = lo_ref[d], hi_ref[d]
        blk_ref[b] = feat_ref[pl.ds(first, CAP), :]
        at, lane0 = first // 128, lax.rem(first, 128)
        turn = lax.rem(128 - lane0, 128)
        live = (pos >= lo) & (pos < hi)

        def moved(ref):
            here = pltpu.roll(ref[pl.ds(at, 8), :], turn, 1)
            after = pltpu.roll(ref[pl.ds(at + 1, 8), :], turn, 1)
            return jnp.where(lane < 128 - lane0, here, after)

        parents, kinds = moved(par), moved(kind)

        def marked(v, other):
            v = jnp.where(live, v, other)
            return jnp.where(pos == 1022, lo, jnp.where(pos == 1023, hi, v))

        slots_ref[b] = marked(kinds * PAR + (parents & (PAR - 1)), SLOTS)
        rows_ref[b] = marked((parents & (NZ * PAR - 1)) + kinds * (NZ * PAR), SLOTS * NZ)
        return c

    lax.fori_loop(0, NZ, block, 0)


def pack(parents, codes, feats):
    rows = feats.shape[0]
    whole = lambda a: pl.BlockSpec(a.shape, lambda i: (0, 0))
    return pl.pallas_call(
        pack_kernel,
        out_shape=(
            jax.ShapeDtypeStruct((NS, CAP, 128), BF16),
            jax.ShapeDtypeStruct((NS, 8, 128), I32),
            jax.ShapeDtypeStruct((NS, 8, 128), I32),
        )
        + (jax.ShapeDtypeStruct((NS,), I32),) * 3,
        grid=(NY,),
        in_specs=[whole(parents), whole(codes), whole(feats)],
        out_specs=(
            pl.BlockSpec((NZ, CAP, 128), lambda i: (i, 0, 0)),
            pl.BlockSpec((NZ, 8, 128), lambda i: (i, 0, 0)),
            pl.BlockSpec((NZ, 8, 128), lambda i: (i, 0, 0)),
            SM,
            SM,
            SM,
        ),
        scratch_shapes=[pltpu.VMEM((rows // 128 + 16, 128), I32), pltpu.VMEM((rows // 128 + 16, 128), I32)],
        compiler_params=pltpu.CompilerParams(vmem_limit_bytes=VLIM),
        cost_estimate=cost(8),
        name="pack",
    )(parents, codes, feats)


def exchange_kernel(grad_ref, rows_ref, slots_ref, blk_ref, table_ref, want_ref, got_ref, *rest):
    parts, (ss, rs, ys, yr, gs, gr, fs, fr, local) = rest[:NZ], rest[NZ:]
    dp, me = lax.axis_index("dp"), lax.axis_index("space")
    y, z = me // NZ, lax.rem(me, NZ)
    barrier = pltpu.get_barrier_semaphore()

    def greet(i, c):
        pl.semaphore_signal(barrier, inc=1, device_id=(dp, lax.rem(me + i, NS)), device_id_type=MESH)
        return c

    lax.fori_loop(1, NS, greet, 0)
    own = [
        pltpu.make_async_copy(grad_ref, table_ref.at[z], local.at[0]),
        pltpu.make_async_copy(rows_ref.at[pl.ds(y * NZ, NZ)], want_ref.at[pl.ds(y * NZ, NZ)], local.at[1]),
        pltpu.make_async_copy(slots_ref.at[me], got_ref.at[me], local.at[2]),
    ]
    for r, part in enumerate(parts):
        own.append(pltpu.make_async_copy(blk_ref.at[y * NZ + lax.rem(z + r, NZ)], part.at[y], local.at[3 + r]))
    for copy in own:
        copy.start()
    pl.semaphore_wait(barrier, NS - 1)
    half = PAR // 2

    def hop(k, side, sub):
        block = lax.rem(z - k + NZ, NZ) if side == 0 else lax.rem(z + k, NZ)
        to = lax.rem(z + 1, NZ) if side == 0 else lax.rem(z + NZ - 1, NZ)
        part = pl.ds(sub * half, half)
        src = grad_ref.at[part] if k == 0 else table_ref.at[block, part]
        return pltpu.make_async_remote_copy(
            src,
            table_ref.at[block, part],
            ss.at[side, k, sub],
            rs.at[side, k, sub],
            device_id=(dp, y * NZ + to),
            device_id_type=MESH,
        )

    chain = [(k, i) for k in range(4) for i in range(2 if k < 3 else 1)]
    hops = {(k, side, i): hop(k, side, side ^ i) for k, i in chain for side in range(2)}

    def rows_to(i):
        ty = lax.rem(y + i, NY)
        return pltpu.make_async_remote_copy(
            rows_ref.at[pl.ds(ty * NZ, NZ)],
            want_ref.at[pl.ds(y * NZ, NZ)],
            ys.at[i],
            yr.at[i],
            device_id=(dp, ty * NZ + z),
            device_id_type=MESH,
        )

    def block_to(i, r):
        ty = lax.rem(y + i, NY)
        return pltpu.make_async_remote_copy(
            blk_ref.at[ty * NZ + lax.rem(z + r, NZ)],
            parts[r].at[y],
            fs.at[i, r],
            fr.at[i, r],
            device_id=(dp, ty * NZ + z),
            device_id_type=MESH,
        )

    moves = [block_to(i, r) for r in range(NZ) for i in range(1, NY)]

    def slots_to(i):
        t = lax.rem(me + i, NS)
        return pltpu.make_async_remote_copy(
            slots_ref.at[t], got_ref.at[me], gs.at[i], gr.at[i], device_id=(dp, t), device_id_type=MESH
        )

    for i in range(2):
        for side in range(2):
            hops[0, side, i].start()
    for i in range(1, NY):
        rows_to(i).start()

    def start_slots(i, c):
        slots_to(i).start()
        return c

    lax.fori_loop(1, NS, start_slots, 0)
    for move in moves:
        move.start()
    for k, i in chain:
        for side in range(2):
            hops[k, side, i].wait_recv()
            if (k + 1, side, i) in hops:
                hops[k + 1, side, i].start()
    for copy in hops.values():
        copy.wait_send()
    for move in moves:
        move.wait()
    for i in range(1, NY):
        rows_to(i).wait()

    def end_slots(i, c):
        slots_to(i).wait()
        return c

    lax.fori_loop(1, NS, end_slots, 0)
    for copy in own:
        copy.wait()


def exchange(grad, rows, slots, blocks):
    ints = jax.ShapeDtypeStruct((NS, 8, 128), I32)
    part = jax.ShapeDtypeStruct((NY, CAP, 128), BF16)
    dma = pltpu.SemaphoreType.DMA
    sems = [(2, 4, 2), (2, 4, 2), (NY,), (NY,), (NS,), (NS,), (NY, NZ), (NY, NZ), (3 + NZ,)]
    out = pl.pallas_call(
        exchange_kernel,
        out_shape=(jax.ShapeDtypeStruct((NZ, PAR, 128), BF16), ints, ints) + (part,) * NZ,
        in_specs=[ANY] * 4,
        out_specs=(ANY,) * (3 + NZ),
        scratch_shapes=[dma(n) for n in sems],
        compiler_params=pltpu.CompilerParams(collective_id=1, has_side_effects=True),
        cost_estimate=cost(50),
        name="exchange",
    )(grad, rows, slots, blocks)
    return out[0], out[1], out[2], out[3:]


def proxy_kernel(place_ref, want_ref, codes_ref, table_ref, weight_ref, *rest):
    parts, outs = rest[:NZ], rest[NZ : NZ + NY]
    term_ref, wide, rowbuf, feats, acc, sems = rest[NZ + NY :]
    y, z = place_ref[0], place_ref[1]
    copies = [pltpu.make_async_copy(part, feats.at[r], sems.at[r]) for r, part in enumerate(parts)]
    for copy in copies:
        copy.start()
    acc[...] = jnp.zeros(acc.shape, F32)

    def widen(i, c):
        at = pl.ds(pl.multiple_of(i * 512, 512), 512)
        wide[at, :] = table_ref[at, :].astype(F32)
        return c

    lax.fori_loop(0, NZ * PAR // 512, widen, 0)
    for copy in copies:
        copy.wait()

    for i, out_ref in enumerate(outs):
        q = (y + i) & (NY - 1)

        def block(r, c, q=q, out_ref=out_ref):
            zz = (z + r) & (NZ - 1)
            at = q * NZ + zz
            base = at * 1024
            lo, hi = want_ref[base + 1022], want_ref[base + 1023]

            def group(g, c):
                for u in range(16):
                    j = g * 16 + u
                    rowbuf[pl.ds(j, 1), :] = wide[pl.ds(want_ref[base + j] & (NZ * PAR - 1), 1), :]
                return c

            lax.fori_loop(lo // 16, (hi + 15) // 16, group, 0)
            codes = jnp.transpose((codes_ref[at] >> 14).astype(F32))

            def piece(first, last):
                cols = range(first // 128, (last + 127) // 128)
                kinds = [jnp.broadcast_to(codes[: min(128, last - m * 128), m : m + 1], (min(128, last - m * 128), 128)) for m in cols]
                kinds = jnp.concatenate(kinds, axis=0)
                rows = rowbuf[first:last, :]
                none = jnp.zeros(rows.shape, F32)
                placed = [jnp.where(kinds == k, rows, none).astype(BF16) for k in range(KINDS)]
                placed = jnp.concatenate(placed, axis=1)
                grads = jnp.dot(placed, weight_ref[...], preferred_element_type=F32)
                out_ref[zz, first:last, :] = grads.astype(BF16)
                turned = jnp.transpose(feats[r, q, first:last, :])
                acc[...] += jnp.dot(turned, placed, preferred_element_type=F32)

            piece(0, 256)

            @pl.when(hi > 256)
            def _():
                piece(256, CAP)

            return c

        lax.fori_loop(0, NZ, block, 0)
    for k in range(KINDS):
        part = slice(k * 128, (k + 1) * 128)
        term_ref[part, :] = acc[:, part]


def proxy(place, want, table, weight, parts):
    return pl.pallas_call(
        proxy_kernel,
        out_shape=(jax.ShapeDtypeStruct((NZ, CAP, 128), BF16),) * NY
        + (jax.ShapeDtypeStruct((KINDS * 128, 128), F32),),
        in_specs=[SM, SM, VM, VM, VM] + [ANY] * NZ,
        out_specs=(VM,) * (NY + 1),
        scratch_shapes=[
            pltpu.VMEM((NZ * PAR, 128), F32),
            pltpu.VMEM((CAP, 128), F32),
            pltpu.VMEM((NZ, NY, CAP, 128), BF16),
            pltpu.VMEM((128, KINDS * 128), F32),
            pltpu.SemaphoreType.DMA((NZ,)),
        ],
        compiler_params=pltpu.CompilerParams(vmem_limit_bytes=VLIM),
        cost_estimate=cost(30),
        name="proxy",
    )(place, want.reshape(-1), want, table, weight, *parts)


def owner_kernel(place_ref, slot_ref, weight_ref, *rest):
    parts = rest[:NZ]
    out_ref, grid_ref, rowbuf, feats, sems = rest[NZ:]
    z = place_ref[1]
    copies = [pltpu.make_async_copy(part, feats.at[s], sems.at[s]) for s, part in enumerate(parts)]
    for copy in copies:
        copy.start()

    def clear(i, c):
        grid_ref[pl.ds(pl.multiple_of(i * 512, 512), 512), :] = jnp.zeros((512, 128), F32)
        return c

    lax.fori_loop(0, SLOTS // 512, clear, 0)

    for s in range(NZ):
        copies[s].wait()

        def block(q, c, s=s):
            base = (q * NZ + ((z - s) & (NZ - 1))) * 1024
            lo, hi = slot_ref[base + 1022], slot_ref[base + 1023]
            rowbuf[...] = feats[s, q].astype(F32)

            def group(g, c):
                for u in range(16):
                    j = g * 16 + u
                    grid_ref[pl.ds(slot_ref[base + j], 1), :] = rowbuf[pl.ds(j, 1), :]
                return c

            lax.fori_loop(lo // 16, (hi + 15) // 16, group, 0)
            return c

        lax.fori_loop(0, NY, block, 0)

    def chunk(i, c):
        total = jnp.zeros((512, 128), F32)
        for k in range(0, KINDS, 2):
            pair = [grid_ref[pl.ds(pl.multiple_of(m * PAR + i * 512, 512), 512), :].astype(BF16) for m in (k, k + 1)]
            kids = jnp.concatenate(pair, axis=1)
            total = total + jnp.dot(kids, weight_ref[k * 128 : (k + 2) * 128, :], preferred_element_type=F32)
        out_ref[pl.ds(pl.multiple_of(i * 512, 512), 512), :] = total.astype(BF16)
        return c

    lax.fori_loop(0, PAR // 512, chunk, 0)


def owner(place, slots, weight, parts):
    return pl.pallas_call(
        owner_kernel,
        out_shape=jax.ShapeDtypeStruct((PAR, 128), BF16),
        in_specs=[SM, SM, VM] + [ANY] * NZ,
        out_specs=VM,
        scratch_shapes=[
            pltpu.VMEM((SLOTS + 8, 128), F32),
            pltpu.VMEM((CAP, 128), F32),
            pltpu.VMEM((NZ, NY, CAP, 128), BF16),
            pltpu.SemaphoreType.DMA((NZ,)),
        ],
        compiler_params=pltpu.CompilerParams(vmem_limit_bytes=VLIM),
        cost_estimate=cost(18),
        name="owner",
    )(place, slots.reshape(-1), weight, *parts)


def total_kernel(scale, term_ref, out_ref, b1, s1, b2, s2, b3, s3, b4, s4, send, recv):
    dp, me = lax.axis_index("dp"), lax.axis_index("space")
    y, z = me // NZ, lax.rem(me, NZ)
    at_dp = lambda i: (lax.rem(dp + i, ND), me)
    at_z = lambda i: (dp, y * NZ + lax.rem(z + i, NZ))
    at_y = lambda i: (dp, lax.rem(y + i, NY) * NZ + z)
    barrier = pltpu.get_barrier_semaphore()
    for who, n in ((at_dp, ND), (at_z, NZ), (at_y, NY)):
        for i in range(1, n):
            pl.semaphore_signal(barrier, inc=1, device_id=who(i), device_id_type=MESH)
    pl.semaphore_wait(barrier, ND + NZ + NY - 3)

    def swap(phase, n, who, src, dst):
        copies = [
            pltpu.make_async_remote_copy(
                src(i), dst, send.at[phase, i], recv.at[phase, i], device_id=who(i), device_id_type=MESH
            )
            for i in range(1, n)
        ]
        for c in copies:
            c.start()
        return copies

    def end(copies):
        for c in copies:
            c.wait()

    def rows(i, n):
        return pl.ds(pl.multiple_of(i * n, n), n)

    c = swap(0, ND, at_dp, lambda i: term_ref.at[rows(lax.rem(dp + i, ND), 128)], b1.at[dp])
    b1[dp] = term_ref[rows(dp, 128), :]
    end(c)
    s1[...] = ((b1[0] + b1[1]) + (b1[2] + b1[3])) + ((b1[4] + b1[5]) + (b1[6] + b1[7]))
    c = swap(1, NZ, at_z, lambda i: s1.at[rows(lax.rem(z + i, NZ), 16)], b2.at[z])
    b2[z] = s1[rows(z, 16), :]
    end(c)
    s2[...] = ((b2[0] + b2[1]) + (b2[2] + b2[3])) + ((b2[4] + b2[5]) + (b2[6] + b2[7]))
    c = swap(2, NY, at_y, lambda i: s2, b3.at[y])
    b3[y] = s2[...]
    end(c)
    s3[...] = ((b3[0] + b3[1]) + (b3[2] + b3[3])) * scale
    c = swap(3, NZ, at_z, lambda i: s3, b4.at[rows(z, 16)])
    b4[rows(z, 16), :] = s3[...]
    end(c)
    c = swap(4, ND, at_dp, lambda i: b4, s4.at[rows(dp, 128)])
    s4[rows(dp, 128), :] = b4[...]
    end(c)
    out_ref[...] = s4[...]


def total(term, scale):
    n = KINDS * 128
    return pl.pallas_call(
        lambda *refs: total_kernel(scale, *refs),
        out_shape=jax.ShapeDtypeStruct((n, 128), F32),
        in_specs=[VM],
        out_specs=VM,
        scratch_shapes=[
            pltpu.VMEM((ND, 128, 128), F32),
            pltpu.VMEM((128, 128), F32),
            pltpu.VMEM((NZ, 16, 128), F32),
            pltpu.VMEM((16, 128), F32),
            pltpu.VMEM((NY, 16, 128), F32),
            pltpu.VMEM((16, 128), F32),
            pltpu.VMEM((128, 128), F32),
            pltpu.VMEM((n, 128), F32),
            pltpu.SemaphoreType.DMA((5, 8)),
            pltpu.SemaphoreType.DMA((5, 8)),
        ],
        compiler_params=pltpu.CompilerParams(collective_id=2, has_side_effects=True),
        cost_estimate=cost(33),
        name="total",
    )(term)


def unpack_kernel(place_ref, first_ref, lo_ref, hi_ref, b0, b1, b2, b3, out_ref):
    row = lax.broadcasted_iota(I32, (16, 128), 0)
    for i, back_ref in enumerate((b0, b1, b2, b3)):

        def block(b, c, i=i, back_ref=back_ref):
            d = ((place_ref[0] - i) & (NY - 1)) * NZ + b
            first, lo, hi = first_ref[d], lo_ref[d], hi_ref[d]

            def tile(t, c):
                src = pl.ds(pl.multiple_of(t * 16, 16), 16)
                dst = pl.ds(pl.multiple_of(first + t * 16, 16), 16)
                at = row + t * 16
                new, old = back_ref[b, src, :].astype(F32), out_ref[dst, :].astype(F32)
                out_ref[dst, :] = jnp.where((at >= lo) & (at < hi), new, old).astype(BF16)
                return c

            def plain(t, c):
                src = pl.ds(pl.multiple_of(t * 16, 16), 16)
                out_ref[pl.ds(pl.multiple_of(first + t * 16, 16), 16), :] = back_ref[b, src, :]
                return c

            begin, end = (lo + 15) // 16, hi // 16
            lax.fori_loop(begin, end, plain, 0)
            lax.fori_loop(lo // 16, jnp.minimum(lo // 16 + 1, (hi + 15) // 16), tile, 0)
            lax.fori_loop(jnp.maximum(end, lo // 16 + 1), (hi + 15) // 16, tile, 0)
            return c

        lax.fori_loop(0, NZ, block, 0)


def unpack(place, first, lo, hi, back, rows):
    return pl.pallas_call(
        unpack_kernel,
        out_shape=jax.ShapeDtypeStruct((rows, 128), BF16),
        in_specs=[SM] * 4 + [VM] * NY,
        out_specs=VM,
        compiler_params=pltpu.CompilerParams(vmem_limit_bytes=VLIM),
        cost_estimate=cost(8),
        name="unpack",
    )(place, first, lo, hi, *back)


def per_device(features, child_parent, child_code, weight, out_grad):
    feats, cotangent = features[0], out_grad[0]
    fine_rows = feats.shape[0]
    as2d = lambda v: v.reshape(fine_rows // 128, 128)
    blocks, slots, rows, first, lo, hi = pack(as2d(child_parent[0]), as2d(child_code[0]), feats)
    table, want, got, parts = exchange(cotangent, rows, slots, blocks)
    me = lax.axis_index("space")
    place = jnp.stack([me // NZ, lax.rem(me, NZ)])

    def along_z(v, s):
        if s == 0:
            return v
        return lax.ppermute(v, "space", [(d, d // NZ * NZ + (d + s) % NZ) for d in range(NS)])

    def along_y(v, i):
        if i == 0:
            return v
        return lax.ppermute(v, "space", [(d, (d + i * NZ) % NS) for d in range(NS)])

    arrived = [along_z(v, s) for s, v in enumerate(parts)]
    weight_back = jnp.transpose(weight, (0, 2, 1)).reshape(KINDS * 128, 128)
    *reply, term = proxy(place, want, table.reshape(NZ * PAR, 128), weight_back, parts)
    back = [along_y(v, i) for i, v in enumerate(reply)]
    grad_rows = fine_rows * NS * lax.axis_size("dp")
    weight_grad = total(term, float(1.0 / grad_rows**0.5))
    first, weight_grad = lax.optimization_barrier((first, weight_grad))
    feature_grad = unpack(place, first, lo, hi, back, fine_rows)
    got, feature_grad = lax.optimization_barrier((got, feature_grad))
    result = owner(place, got, weight.reshape(KINDS * 128, 128), arrived)
    return result[None], feature_grad[None], weight_grad.reshape(KINDS, 128, 128)


def solution(mesh):
    placed = (P("dp", "space", None), P("dp", "space"), P("dp", "space"), P(), P("dp", "space", None))
    return jax.shard_map(
        per_device,
        mesh=mesh,
        in_specs=placed,
        out_specs=(P("dp", "space", None), P("dp", "space", None), P()),
        check_vma=False,
    )
```

profile of v0, /device:TPU:2, one launch (start us, length us, event | category | flops | bytes accessed | tf_op | source)
XLA Modules:
  0.0 307.8 jit_solution(8045186048231962984)
XLA Ops:
  0.6 1.8 copy.8
  2.4 0.6 pad_add_fusion.place_ref
  3.1 6.1 %pack.1 = (bf16[32,528,128]{2,1,0:T(8,128)(2,1)}, s32[32,8,128]{2,1,0:T(8,128)}, s32[32,8,128]{2,1,0:T(8,128)}, s32[32]{0:T(128)}, s32[32]{0:T(128)}, /*index=5*/s32[32]{0:T(128)}) custom-call(s32[64,128]{1,0:T(8,128)} %bitcast.26, s32[64,128]{1,0:T(8,128)} %bitcast.27, bf16[8192,128]{1,0:T(8,128)(2,1)} %bitcast.16), custom_call_target="tpu_custom_call" | custom-call | bytes 28800000 | tf_op jit(solution)/shard_map/pack/pallas_call | solution.py:83
  9.2 63.1 %exchange.1 = (bf16[8,2048,128]{2,1,0:T(8,128)(2,1)}, s32[32,8,128]{2,1,0:T(8,128)}, s32[32,8,128]{2,1,0:T(8,128)}, bf16[4,528,128]{2,1,0:T(8,128)(2,1)}, bf16[4...) custom-call(bf16[2048,128]{1,0:T(8,128)(2,1)} %bitcast.23, ...), custom_call_target="tpu_custom_call" | custom-call | bytes 180000000 | tf_op jit(solution)/shard_map/exchange/pallas_call | solution.py:217
  72.3 43.2 %proxy.1 = (bf16[8,528,128]{2,1,0:T(8,128)(2,1)}, bf16[8,528,128]{2,1,0:T(8,128)(2,1)}, bf16[8,528,128]{2,1,0:T(8,128)(2,1)}, bf16[8,528,128]{2,1,0:T(8,128)(2,1)}, f32[1024,128]{1,0:T(8,128)}) custom-call(s32[2]{0:T(128)} %pad_add_fusion.place_ref, s32[32768]{0:T(1024)} %bitcast.22, s32[32,8,128]{2,1,0:T(8,128)} %get-tuple-element.34.codes_ref, ...), custom_call_target="tpu_custom_call" | custom-call | bytes 108000000 | tf_op jit(solution)/shard_map/proxy/pallas_call | solution.py:294
  115.5 3.5 %collective-permute-start = (bf16[8,528,128]{2,1,0:T(8,128)(2,1)}, bf16[8,528,128]{2,1,0:T(8,128)(2,1)S(1)}, u32[]{:S(2)}, u32[]{:S(2)}) collective-permute-start(bf16[8,528,128]{2,1,0:T(8,128)(2,1)} %get-tuple-element.49), channel_id=1, source_target_pairs={{0,8},{1,9},{2,10},{3,11},{4,12},{5,13},{6,14},{7,15},{8,16},{9,17... | collective-permute-start | bytes 3244040 | tf_op jit(solution)/shard_map/ppermute | solution.py:511
  118.9 2.2 collective-permute-start.1
  121.1 1.9 collective-permute-start.2
  123.1 0.1 collective-permute-start.3
  123.2 2.4 collective-permute-start.4
  125.7 18.7 %collective-permute-done.3.rest_1_ = bf16[4,528,128]{2,1,0:T(8,128)(2,1)S(1)} collective-permute-done((bf16[4,528,128]{2,1,0:T(8,128)(2,1)}, bf16[4,528,128]{2,1,0:T(8,128)(2,1)S(1)}, u32[]{:S(2)}, u32[]{:S(2)}) %collective-permute-start.3) | collective-permute-done | bytes 540704 | tf_op jit(solution)/shard_map/ppermute | solution.py:506
  144.3 20.1 %collective-permute-done.4.rest_2_ = bf16[4,528,128]{2,1,0:T(8,128)(2,1)S(1)} collective-permute-done((bf16[4,528,128]{2,1,0:T(8,128)(2,1)S(1)}, bf16[4,528,128]{2,1,0:T(8,128)(2,1)S(1)}, u32[]{:S(2)}, u32[]{:S(2)}) %collective-permute-start.4) | collective-permute-done | bytes 540704 | tf_op jit(solution)/shard_map/ppermute | solution.py:506
  164.5 6.5 %collective-permute-start.6 = (bf16[4,528,128]{2,1,0:T(8,128)(2,1)}, bf16[4,528,128]{2,1,0:T(8,128)(2,1)}, u32[]{:S(2)}, u32[]{:S(2)}) collective-permute-start(bf16[4,528,128]{2,1,0:T(8,128)(2,1)} %get-tuple-element.40.rest_4_), channel_id=1, source_target_pairs={{0,4},{1,5},{2,6},{3,7},{4,0},{5,1},{6,2},{7,3},{8,12},{9,13},{10,... | collective-permute-start | bytes 1622024 | tf_op jit(solution)/shard_map/ppermute | solution.py:506
  171.0 0.0 collective-permute-done.b1
  171.0 8.8 %collective-permute-start.7 = (bf16[4,528,128]{2,1,0:T(8,128)(2,1)}, bf16[4,528,128]{2,1,0:T(8,128)(2,1)}, u32[]{:S(2)}, u32[]{:S(2)}) collective-permute-start(bf16[4,528,128]{2,1,0:T(8,128)(2,1)} %get-tuple-element.41.rest_5_), channel_id=1, source_target_pairs={{0,5},{1,6},{2,7},{3,0},{4,1},{5,2},{6,3},{7,4},{8,13},{9,14},{10,... | collective-permute-start | bytes 1622024 | tf_op jit(solution)/shard_map/ppermute | solution.py:506
  179.8 0.0 collective-permute-done.1.b2
  179.8 0.0 collective-permute-done.2.b3
  179.8 0.7 collective-permute-start.9
  180.5 98.2 %total.1 = f32[1024,128]{1,0:T(8,128)} custom-call(f32[1024,128]{1,0:T(8,128)} %get-tuple-element.44.refs_0_), custom_call_target="tpu_custom_call" | custom-call | bytes 118800000 | tf_op jit(solution)/shard_map/total/pallas_call | solution.py:429
  278.8 9.2 %unpack.1 = bf16[8192,128]{1,0:T(8,128)(2,1)} custom-call(s32[2]{0:T(128)} %pad_add_fusion.place_ref, s32[32]{0:T(128)} %get-tuple-element.45.first_ref, s32[32]{0:T(128)} %get-tuple-element.46.lo_ref, s32[32]{0:T(128)} %get-tuple-element.47.hi_ref, bf16[8,528,128]{2,1,0:T(8,128)(2,1)} %get-tuple-element.48.b0, bf16[8,528,128]{2,1,0:T(8,128)(2,1)} %copy-done.1, ...), custom_call_target="tpu_custom_call" | custom-call | bytes 28800000 | tf_op jit(solution)/shard_map/unpack/pallas_call | solution.py:483
  288.0 0.0 collective-permute-done.5.rest_3_
  288.0 0.0 collective-permute-done.6.rest_4_
  288.0 18.9 %owner.1 = bf16[2048,128]{1,0:T(8,128)(2,1)} custom-call(s32[2]{0:T(128)} %pad_add_fusion.place_ref, s32[32768]{0:T(1024)} %bitcast.25, bf16[1024,128]{1,0:T(8,128)(2,1)} %bitcast.21, bf16[4,528,128]{2,1,0:T(8,128)(2,1)} %get-tuple-element.36.rest_0_, bf16[4,528,128]{2,1,0:T(8,128)(2,1)} %copy-done.5, bf16[4,528,128]{2,1,0:T(8,128)(2,1)} %copy-done.6, ...), custom_call_target="tpu_custom_call" | custom-call | bytes 64800000 | tf_op jit(solution)/shard_map/owner/pallas_call | solution.py:359
  307.0 0.8 copy.10
  (19 shorter events, 0.0 us)
Async XLA Ops:
  72.3 50.9 %copy-start.4 = (bf16[4,528,128]{2,1,0:T(8,128)(2,1)S(1)}, bf16[4,528,128]{2,1,0:T(8,128)(2,1)}, u32[]{:S(2)}) copy-start(bf16[4,528,128]{2,1,0:T(8,128)(2,1)} %get-tuple-element.38.rest_2_) | copy-start | bytes 1622020
  115.5 55.5 %collective-permute-start = (bf16[8,528,128]{2,1,0:T(8,128)(2,1)}, bf16[8,528,128]{2,1,0:T(8,128)(2,1)S(1)}, u32[]{:S(2)}, u32[]{:S(2)}) collective-permute-start(bf16[8,528,128]{2,1,0:T(8,128)(2,1)} %get-tuple-element.49), channel_id=1, source_target_pairs={{0,8},{1,9},{2,10},{3,11},{4,12},{5,13},{6,14},{7,15},{8,16},{9,17... | collective-permute-start | bytes 3244040 | tf_op jit(solution)/shard_map/ppermute | solution.py:511
  118.9 60.9 %collective-permute-start.1 = (bf16[8,528,128]{2,1,0:T(8,128)(2,1)}, bf16[8,528,128]{2,1,0:T(8,128)(2,1)S(1)}, u32[]{:S(2)}, u32[]{:S(2)}) collective-permute-start(bf16[8,528,128]{2,1,0:T(8,128)(2,1)} %get-tuple-element.50), channel_id=1, source_target_pairs={{0,16},{1,17},{2,18},{3,19},{4,20},{5,21},{6,22},{7,23},{8,24},{9,... | collective-permute-start | bytes 3244040 | tf_op jit(solution)/shard_map/ppermute | solution.py:511
  121.1 58.7 %collective-permute-start.2 = (bf16[8,528,128]{2,1,0:T(8,128)(2,1)}, bf16[8,528,128]{2,1,0:T(8,128)(2,1)S(1)}, u32[]{:S(2)}, u32[]{:S(2)}) collective-permute-start(bf16[8,528,128]{2,1,0:T(8,128)(2,1)} %get-tuple-element.51), channel_id=1, source_target_pairs={{0,24},{1,25},{2,26},{3,27},{4,28},{5,29},{6,30},{7,31},{8,0},{9,1... | collective-permute-start | bytes 3244040 | tf_op jit(solution)/shard_map/ppermute | solution.py:511
  123.1 21.3 %collective-permute-start.3 = (bf16[4,528,128]{2,1,0:T(8,128)(2,1)}, bf16[4,528,128]{2,1,0:T(8,128)(2,1)S(1)}, u32[]{:S(2)}, u32[]{:S(2)}) collective-permute-start(bf16[4,528,128]{2,1,0:T(8,128)(2,1)} %get-tuple-element.37.rest_1_), channel_id=1, source_target_pairs={{0,1},{1,2},{2,3},{3,4},{4,5},{5,6},{6,7},{7,0},{8,9},{9,10},{10,1... | collective-permute-start | bytes 1622024 | tf_op jit(solution)/shard_map/ppermute | solution.py:506
  123.2 41.2 %collective-permute-start.4 = (bf16[4,528,128]{2,1,0:T(8,128)(2,1)S(1)}, bf16[4,528,128]{2,1,0:T(8,128)(2,1)S(1)}, u32[]{:S(2)}, u32[]{:S(2)}) collective-permute-start(bf16[4,528,128]{2,1,0:T(8,128)(2,1)S(1)} %copy-done.4), channel_id=1, source_target_pairs={{0,2},{1,3},{2,4},{3,5},{4,6},{5,7},{6,0},{7,1},{8,10},{9,11},{10,... | collective-permute-start | bytes 1622024 | tf_op jit(solution)/shard_map/ppermute | solution.py:506
  144.3 35.5 %copy-start.5 = (bf16[4,528,128]{2,1,0:T(8,128)(2,1)}, bf16[4,528,128]{2,1,0:T(8,128)(2,1)S(1)}, u32[]{:S(2)}) copy-start(bf16[4,528,128]{2,1,0:T(8,128)(2,1)S(1)} %collective-permute-done.3.rest_1_) | copy-start | bytes 1622020
  144.3 143.6 %collective-permute-start.5 = (bf16[4,528,128]{2,1,0:T(8,128)(2,1)}, bf16[4,528,128]{2,1,0:T(8,128)(2,1)}, u32[]{:S(2)}, u32[]{:S(2)}) collective-permute-start(bf16[4,528,128]{2,1,0:T(8,128)(2,1)} %get-tuple-element.39.rest_3_), channel_id=1, source_target_pairs={{0,3},{1,4},{2,5},{3,6},{4,7},{5,0},{6,1},{7,2},{8,11},{9,12},{10,... | collective-permute-start | bytes 1622024 | tf_op jit(solution)/shard_map/ppermute | solution.py:506
  164.4 16.1 %copy-start.6 = (bf16[4,528,128]{2,1,0:T(8,128)(2,1)}, bf16[4,528,128]{2,1,0:T(8,128)(2,1)S(1)}, u32[]{:S(2)}) copy-start(bf16[4,528,128]{2,1,0:T(8,128)(2,1)S(1)} %collective-permute-done.4.rest_2_) | copy-start | bytes 1622020
  164.5 123.5 %collective-permute-start.6 = (bf16[4,528,128]{2,1,0:T(8,128)(2,1)}, bf16[4,528,128]{2,1,0:T(8,128)(2,1)}, u32[]{:S(2)}, u32[]{:S(2)}) collective-permute-start(bf16[4,528,128]{2,1,0:T(8,128)(2,1)} %get-tuple-element.40.rest_4_), channel_id=1, source_target_pairs={{0,4},{1,5},{2,6},{3,7},{4,0},{5,1},{6,2},{7,3},{8,12},{9,13},{10,... | collective-permute-start | bytes 1622024 | tf_op jit(solution)/shard_map/ppermute | solution.py:506
  171.0 107.7 %copy-start.1 = (bf16[8,528,128]{2,1,0:T(8,128)(2,1)}, bf16[8,528,128]{2,1,0:T(8,128)(2,1)S(1)}, u32[]{:S(2)}) copy-start(bf16[8,528,128]{2,1,0:T(8,128)(2,1)S(1)} %collective-permute-done.b1) | copy-start | bytes 3244036
  171.0 117.0 %collective-permute-start.7 = (bf16[4,528,128]{2,1,0:T(8,128)(2,1)}, bf16[4,528,128]{2,1,0:T(8,128)(2,1)}, u32[]{:S(2)}, u32[]{:S(2)}) collective-permute-start(bf16[4,528,128]{2,1,0:T(8,128)(2,1)} %get-tuple-element.41.rest_5_), channel_id=1, source_target_pairs={{0,5},{1,6},{2,7},{3,0},{4,1},{5,2},{6,3},{7,4},{8,13},{9,14},{10,... | collective-permute-start | bytes 1622024 | tf_op jit(solution)/shard_map/ppermute | solution.py:506
  179.8 99.0 %copy-start.2 = (bf16[8,528,128]{2,1,0:T(8,128)(2,1)}, bf16[8,528,128]{2,1,0:T(8,128)(2,1)S(1)}, u32[]{:S(2)}) copy-start(bf16[8,528,128]{2,1,0:T(8,128)(2,1)S(1)} %collective-permute-done.1.b2) | copy-start | bytes 3244036
  179.8 108.2 %collective-permute-start.8 = (bf16[4,528,128]{2,1,0:T(8,128)(2,1)}, bf16[4,528,128]{2,1,0:T(8,128)(2,1)}, u32[]{:S(2)}, u32[]{:S(2)}) collective-permute-start(bf16[4,528,128]{2,1,0:T(8,128)(2,1)} %get-tuple-element.42.rest_6_), channel_id=1, source_target_pairs={{0,6},{1,7},{2,0},{3,1},{4,2},{5,3},{6,4},{7,5},{8,14},{9,15},{10,... | collective-permute-start | bytes 1622024 | tf_op jit(solution)/shard_map/ppermute | solution.py:506
  179.8 98.9 %copy-start.3 = (bf16[8,528,128]{2,1,0:T(8,128)(2,1)}, bf16[8,528,128]{2,1,0:T(8,128)(2,1)S(1)}, u32[]{:S(2)}) copy-start(bf16[8,528,128]{2,1,0:T(8,128)(2,1)S(1)} %collective-permute-done.2.b3) | copy-start | bytes 3244036
  179.8 108.2 %collective-permute-start.9 = (bf16[4,528,128]{2,1,0:T(8,128)(2,1)}, bf16[4,528,128]{2,1,0:T(8,128)(2,1)}, u32[]{:S(2)}, u32[]{:S(2)}) collective-permute-start(bf16[4,528,128]{2,1,0:T(8,128)(2,1)} %get-tuple-element.43.rest_7_), channel_id=1, source_target_pairs={{0,7},{1,0},{2,1},{3,2},{4,3},{5,4},{6,5},{7,6},{8,15},{9,8},{10,9... | collective-permute-start | bytes 1622024 | tf_op jit(solution)/shard_map/ppermute | solution.py:506
  288.0 19.0 %copy-start = (f32[1024,128]{1,0:T(8,128)S(1)}, f32[1024,128]{1,0:T(8,128)}, u32[]{:S(2)}) copy-start(f32[1024,128]{1,0:T(8,128)} %total.1) | copy-start | bytes 1572868
where the time goes:
time: 313 us; the launch traced here: 308 us
  Pallas kernels  239 us (76%)
  waiting for transfers between devices  38.8 us (12%)
  starting transfers between devices  26.2 us (8%)
    pallas_call x1, Pallas kernels, total(): pl.pallas_call(lambda *refs: total_kernel(scale, *refs), out_shape=jax.Sh...  98.2 us
    pallas_call x1, Pallas kernels, exchange(): pl.pallas_call(exchange_kernel, out_shape=(jax.ShapeDtypeStruct((NZ, PAR,...  63.1 us
    pallas_call x1, Pallas kernels, proxy(): pl.pallas_call(proxy_kernel, out_shape=(jax.ShapeDtypeStruct((NZ, CAP, 12...  43.2 us
    ppermute x7, waiting for transfers between devices, along_z(): lax.ppermute(v, 'space', [(d, d // NZ * NZ + (d + s) % NZ) for d in range...  38.8 us
    pallas_call x1, Pallas kernels, owner(): pl.pallas_call(owner_kernel, out_shape=jax.ShapeDtypeStruct((PAR, 128), B...  18.9 us
    ppermute x7, starting transfers between devices, along_z(): lax.ppermute(v, 'space', [(d, d // NZ * NZ + (d + s) % NZ) for d in range...  18.6 us
    pallas_call x1, Pallas kernels, unpack(): pl.pallas_call(unpack_kernel, out_shape=jax.ShapeDtypeStruct((rows, 128),...  9.2 us
    ppermute x3, starting transfers between devices, along_y(): return lax.ppermute(v, 'space', [(d, (d + i * NZ) % NS) for d in range(NS)])  7.61 us
  transfers between devices with their start and end apart: 10, of which 2 were waited for; matrix products, arithmetic and copies ran while one was open for 0% of the time, Pallas kernels for 35%

commit v1 on v0

--- a/solution.py
+++ b/solution.py
@@ -106,7 +106,7 @@
 
 
 def exchange_kernel(grad_ref, rows_ref, slots_ref, blk_ref, table_ref, want_ref, got_ref, *rest):
-    parts, (ss, rs, ys, yr, gs, gr, fs, fr, local) = rest[:NZ], rest[NZ:]
+    parts, (mine, ss, rs, ys, yr, gs, gr, fs, fr, local, stage) = rest[:NZ], rest[NZ:]
     dp, me = lax.axis_index("dp"), lax.axis_index("space")
     y, z = me // NZ, lax.rem(me, NZ)
     barrier = pltpu.get_barrier_semaphore()
@@ -121,9 +121,9 @@
         pltpu.make_async_copy(rows_ref.at[pl.ds(y * NZ, NZ)], want_ref.at[pl.ds(y * NZ, NZ)], local.at[1]),
         pltpu.make_async_copy(slots_ref.at[me], got_ref.at[me], local.at[2]),
     ]
-    for r, part in enumerate(parts):
-        own.append(pltpu.make_async_copy(blk_ref.at[y * NZ + lax.rem(z + r, NZ)], part.at[y], local.at[3 + r]))
-    for copy in own:
+    loads = [pltpu.make_async_copy(blk_ref.at[y * NZ + lax.rem(z + r, NZ)], mine.at[r], stage.at[r]) for r in range(NZ)]
+    stores = [pltpu.make_async_copy(mine.at[r], parts[r].at[y], local.at[3 + r]) for r in range(NZ)]
+    for copy in own + loads:
         copy.start()
     pl.semaphore_wait(barrier, NS - 1)
     half = PAR // 2
@@ -188,6 +188,9 @@
     lax.fori_loop(1, NS, start_slots, 0)
     for move in moves:
         move.start()
+    for load, put in zip(loads, stores):
+        load.wait()
+        put.start()
     for k, i in chain:
         for side in range(2):
             hops[k, side, i].wait_recv()
@@ -205,7 +208,7 @@
         return c
 
     lax.fori_loop(1, NS, end_slots, 0)
-    for copy in own:
+    for copy in own + stores:
         copy.wait()
 
 
@@ -213,28 +216,40 @@
     ints = jax.ShapeDtypeStruct((NS, 8, 128), I32)
     part = jax.ShapeDtypeStruct((NY, CAP, 128), BF16)
     dma = pltpu.SemaphoreType.DMA
-    sems = [(2, 4, 2), (2, 4, 2), (NY,), (NY,), (NS,), (NS,), (NY, NZ), (NY, NZ), (3 + NZ,)]
+    sems = [(2, 4, 2), (2, 4, 2), (NY,), (NY,), (NS,), (NS,), (NY, NZ), (NY, NZ), (3 + NZ,), (NZ,)]
     out = pl.pallas_call(
         exchange_kernel,
         out_shape=(jax.ShapeDtypeStruct((NZ, PAR, 128), BF16), ints, ints) + (part,) * NZ,
-        in_specs=[ANY] * 4,
-        out_specs=(ANY,) * (3 + NZ),
-        scratch_shapes=[dma(n) for n in sems],
-        compiler_params=pltpu.CompilerParams(collective_id=1, has_side_effects=True),
+        in_specs=[VM] + [ANY] * 3,
+        out_specs=(VM,) + (ANY,) * (2 + NZ),
+        scratch_shapes=[pltpu.VMEM((NZ, CAP, 128), BF16)] + [dma(n) for n in sems],
+        compiler_params=pltpu.CompilerParams(collective_id=1, has_side_effects=True, vmem_limit_bytes=VLIM),
         cost_estimate=cost(50),
         name="exchange",
     )(grad, rows, slots, blocks)
     return out[0], out[1], out[2], out[3:]
 
 
-def proxy_kernel(place_ref, want_ref, codes_ref, table_ref, weight_ref, *rest):
-    parts, outs = rest[:NZ], rest[NZ : NZ + NY]
-    term_ref, wide, rowbuf, feats, acc, sems = rest[NZ + NY :]
-    y, z = place_ref[0], place_ref[1]
-    copies = [pltpu.make_async_copy(part, feats.at[r], sems.at[r]) for r, part in enumerate(parts)]
+def place():
+    me = lax.axis_index("space")
+    return me >> 3, me & (NZ - 1)
+
+
+def proxy_kernel(distances, want_ref, codes_ref, table_ref, weight_ref, *rest):
+    n = len(distances)
+    parts, outs = rest[:NZ], rest[NZ : NZ + n]
+    term_ref, wide, rowbuf, feats, acc, turned_weight, sems = rest[NZ + n :]
+    y, z = place()
+    copies = [
+        pltpu.make_async_copy(part.at[(y + i) & (NY - 1)], feats.at[r, m], sems.at[r, m])
+        for m, i in enumerate(distances)
+        for r, part in enumerate(parts)
+    ]
     for copy in copies:
         copy.start()
     acc[...] = jnp.zeros(acc.shape, F32)
+    for k in range(KINDS):
+        turned_weight[k * 128 : (k + 1) * 128, :] = jnp.transpose(weight_ref[k])
 
     def widen(i, c):
         at = pl.ds(pl.multiple_of(i * 512, 512), 512)
@@ -245,10 +260,10 @@
     for copy in copies:
         copy.wait()
 
-    for i, out_ref in enumerate(outs):
-        q = (y + i) & (NY - 1)
-
-        def block(r, c, q=q, out_ref=out_ref):
+    for m, out_ref in enumerate(outs):
+        q = (y + distances[m]) & (NY - 1)
+
+        def block(r, c, m=m, q=q, out_ref=out_ref):
             zz = (z + r) & (NZ - 1)
             at = q * NZ + zz
             base = at * 1024
@@ -271,9 +286,9 @@
                 none = jnp.zeros(rows.shape, F32)
                 placed = [jnp.where(kinds == k, rows, none).astype(BF16) for k in range(KINDS)]
                 placed = jnp.concatenate(placed, axis=1)
-                grads = jnp.dot(placed, weight_ref[...], preferred_element_type=F32)
+                grads = jnp.dot(placed, turned_weight[...], preferred_element_type=F32)
                 out_ref[zz, first:last, :] = grads.astype(BF16)
-                turned = jnp.transpose(feats[r, q, first:last, :])
+                turned = jnp.transpose(feats[r, m, first:last, :])
                 acc[...] += jnp.dot(turned, placed, preferred_element_type=F32)
 
             piece(0, 256)
@@ -290,30 +305,33 @@
         term_ref[part, :] = acc[:, part]
 
 
-def proxy(place, want, table, weight, parts):
-    return pl.pallas_call(
-        proxy_kernel,
-        out_shape=(jax.ShapeDtypeStruct((NZ, CAP, 128), BF16),) * NY
+def proxy(distances, want, table, weight, parts):
+    n = len(distances)
+    *rows, term = pl.pallas_call(
+        lambda *refs: proxy_kernel(distances, *refs),
+        out_shape=(jax.ShapeDtypeStruct((NZ, CAP, 128), BF16),) * n
         + (jax.ShapeDtypeStruct((KINDS * 128, 128), F32),),
-        in_specs=[SM, SM, VM, VM, VM] + [ANY] * NZ,
-        out_specs=(VM,) * (NY + 1),
+        in_specs=[SM, VM, VM, VM] + [ANY] * NZ,
+        out_specs=(VM,) * (n + 1),
         scratch_shapes=[
             pltpu.VMEM((NZ * PAR, 128), F32),
             pltpu.VMEM((CAP, 128), F32),
-            pltpu.VMEM((NZ, NY, CAP, 128), BF16),
+            pltpu.VMEM((NZ, n, CAP, 128), BF16),
             pltpu.VMEM((128, KINDS * 128), F32),
-            pltpu.SemaphoreType.DMA((NZ,)),
+            pltpu.VMEM((KINDS * 128, 128), BF16),
+            pltpu.SemaphoreType.DMA((NZ, n)),
         ],
         compiler_params=pltpu.CompilerParams(vmem_limit_bytes=VLIM),
-        cost_estimate=cost(30),
+        cost_estimate=cost(20),
         name="proxy",
-    )(place, want.reshape(-1), want, table, weight, *parts)
-
-
-def owner_kernel(place_ref, slot_ref, weight_ref, *rest):
+    )(want.reshape(-1), want, table, weight, *parts)
+    return dict(zip(distances, rows)), term
+
+
+def owner_kernel(slot_ref, weight_ref, *rest):
     parts = rest[:NZ]
     out_ref, grid_ref, rowbuf, feats, sems = rest[NZ:]
-    z = place_ref[1]
+    _, z = place()
     copies = [pltpu.make_async_copy(part, feats.at[s], sems.at[s]) for s, part in enumerate(parts)]
     for copy in copies:
         copy.start()
@@ -355,11 +373,11 @@
     lax.fori_loop(0, PAR // 512, chunk, 0)
 
 
-def owner(place, slots, weight, parts):
+def owner(slots, weight, parts):
     return pl.pallas_call(
         owner_kernel,
         out_shape=jax.ShapeDtypeStruct((PAR, 128), BF16),
-        in_specs=[SM, SM, VM] + [ANY] * NZ,
+        in_specs=[SM, VM] + [ANY] * NZ,
         out_specs=VM,
         scratch_shapes=[
             pltpu.VMEM((SLOTS + 8, 128), F32),
@@ -370,15 +388,16 @@
         compiler_params=pltpu.CompilerParams(vmem_limit_bytes=VLIM),
         cost_estimate=cost(18),
         name="owner",
-    )(place, slots.reshape(-1), weight, *parts)
-
-
-def total_kernel(scale, term_ref, out_ref, b1, s1, b2, s2, b3, s3, b4, s4, send, recv):
+    )(slots.reshape(-1), weight, *parts)
+
+
+def total_kernel(scale, far_ref, near_ref, out_ref, term_ref, b1, s1, b2, s2, b3, s3, b4, s4, send, recv):
     dp, me = lax.axis_index("dp"), lax.axis_index("space")
     y, z = me // NZ, lax.rem(me, NZ)
     at_dp = lambda i: (lax.rem(dp + i, ND), me)
     at_z = lambda i: (dp, y * NZ + lax.rem(z + i, NZ))
     at_y = lambda i: (dp, lax.rem(y + i, NY) * NZ + z)
+    term_ref[...] = far_ref[...] + near_ref[...]
     barrier = pltpu.get_barrier_semaphore()
     for who, n in ((at_dp, ND), (at_z, NZ), (at_y, NY)):
         for i in range(1, n):
@@ -424,14 +443,15 @@
     out_ref[...] = s4[...]
 
 
-def total(term, scale):
+def total(far, near, scale):
     n = KINDS * 128
     return pl.pallas_call(
         lambda *refs: total_kernel(scale, *refs),
         out_shape=jax.ShapeDtypeStruct((n, 128), F32),
-        in_specs=[VM],
+        in_specs=[VM, VM],
         out_specs=VM,
         scratch_shapes=[
+            pltpu.VMEM((n, 128), F32),
             pltpu.VMEM((ND, 128, 128), F32),
             pltpu.VMEM((128, 128), F32),
             pltpu.VMEM((NZ, 16, 128), F32),
@@ -446,15 +466,16 @@
         compiler_params=pltpu.CompilerParams(collective_id=2, has_side_effects=True),
         cost_estimate=cost(33),
         name="total",
-    )(term)
-
-
-def unpack_kernel(place_ref, first_ref, lo_ref, hi_ref, b0, b1, b2, b3, out_ref):
+    )(far, near)
+
+
+def unpack_kernel(first_ref, lo_ref, hi_ref, b0, b1, b2, b3, out_ref):
     row = lax.broadcasted_iota(I32, (16, 128), 0)
+    y, _ = place()
     for i, back_ref in enumerate((b0, b1, b2, b3)):
 
         def block(b, c, i=i, back_ref=back_ref):
-            d = ((place_ref[0] - i) & (NY - 1)) * NZ + b
+            d = ((y - i) & (NY - 1)) * NZ + b
             first, lo, hi = first_ref[d], lo_ref[d], hi_ref[d]
 
             def tile(t, c):
@@ -479,16 +500,16 @@
         lax.fori_loop(0, NZ, block, 0)
 
 
-def unpack(place, first, lo, hi, back, rows):
+def unpack(first, lo, hi, back, rows):
     return pl.pallas_call(
         unpack_kernel,
         out_shape=jax.ShapeDtypeStruct((rows, 128), BF16),
-        in_specs=[SM] * 4 + [VM] * NY,
+        in_specs=[SM] * 3 + [VM] * NY,
         out_specs=VM,
         compiler_params=pltpu.CompilerParams(vmem_limit_bytes=VLIM),
         cost_estimate=cost(8),
         name="unpack",
-    )(place, first, lo, hi, *back)
+    )(first, lo, hi, *back)
 
 
 def per_device(features, child_parent, child_code, weight, out_grad):
@@ -497,8 +518,6 @@
     as2d = lambda v: v.reshape(fine_rows // 128, 128)
     blocks, slots, rows, first, lo, hi = pack(as2d(child_parent[0]), as2d(child_code[0]), feats)
     table, want, got, parts = exchange(cotangent, rows, slots, blocks)
-    me = lax.axis_index("space")
-    place = jnp.stack([me // NZ, lax.rem(me, NZ)])
 
     def along_z(v, s):
         if s == 0:
@@ -511,15 +530,17 @@
         return lax.ppermute(v, "space", [(d, (d + i * NZ) % NS) for d in range(NS)])
 
     arrived = [along_z(v, s) for s, v in enumerate(parts)]
-    weight_back = jnp.transpose(weight, (0, 2, 1)).reshape(KINDS * 128, 128)
-    *reply, term = proxy(place, want, table.reshape(NZ * PAR, 128), weight_back, parts)
-    back = [along_y(v, i) for i, v in enumerate(reply)]
+    table = table.reshape(NZ * PAR, 128)
+    far, far_term = proxy((2, 1), want, table, weight, parts)
+    near, near_term = proxy((3, 0), want, table, weight, parts)
+    reply = {**far, **near}
+    back = [along_y(reply[i], i) for i in range(NY)]
     grad_rows = fine_rows * NS * lax.axis_size("dp")
-    weight_grad = total(term, float(1.0 / grad_rows**0.5))
+    weight_grad = total(far_term, near_term, float(1.0 / grad_rows**0.5))
     first, weight_grad = lax.optimization_barrier((first, weight_grad))
-    feature_grad = unpack(place, first, lo, hi, back, fine_rows)
+    feature_grad = unpack(first, lo, hi, back, fine_rows)
     got, feature_grad = lax.optimization_barrier((got, feature_grad))
-    result = owner(place, got, weight.reshape(KINDS * 128, 128), arrived)
+    result = owner(got, weight.reshape(KINDS * 128, 128), arrived)
     return result[None], feature_grad[None], weight_grad.reshape(KINDS, 128, 128)
 
 

time: 313 us -> 318 us (1.016)
  starting transfers between devices: 26.2 us -> 32.6 us
  Pallas kernels: 239 us -> 243 us
  waiting for transfers between devices: 38.8 us -> 34.9 us
    ppermute x7, starting transfers between devices: 18.6 us -> 25.8 us  [along_z(): lax.ppermute(v, 'space', [(d, d // NZ * NZ + (d + s) % NZ) for d in range...]
    pallas_call x1 -> x2, Pallas kernels: 43.2 us -> 48.2 us  [proxy(): pl.pallas_call(lambda *refs: proxy_kernel(distances, *refs), out_shape=(j...]
    ppermute x7, waiting for transfers between devices: 38.8 us -> 34.9 us  [along_z(): lax.ppermute(v, 'space', [(d, d // NZ * NZ + (d + s) % NZ) for d in range...]
    pallas_call x1, Pallas kernels: 98.2 us -> 94.4 us  [total(): pl.pallas_call(lambda *refs: total_kernel(scale, *refs), out_shape=jax.Sh...]
  transfers between devices with their start and end apart: 10 -> 10, of which waited for: 2 -> 2; matrix products, arithmetic and copies ran while one was open for 0% -> 0% of each run, Pallas kernels for 35% -> 41%
where the time goes in v1:
time: 318 us; the launch traced here: 313 us
  Pallas kernels  243 us (76%)
  waiting for transfers between devices  34.9 us (11%)
  starting transfers between devices  32.6 us (10%)
    pallas_call x1, Pallas kernels, total(): pl.pallas_call(lambda *refs: total_kernel(scale, *refs), out_shape=jax.Sh...  94.4 us
    pallas_call x1, Pallas kernels, exchange(): pl.pallas_call(exchange_kernel, out_shape=(jax.ShapeDtypeStruct((NZ, PAR,...  66 us
    pallas_call x2, Pallas kernels, proxy(): pl.pallas_call(lambda *refs: proxy_kernel(distances, *refs), out_shape=(j...  48.2 us
    ppermute x7, waiting for transfers between devices, along_z(): lax.ppermute(v, 'space', [(d, d // NZ * NZ + (d + s) % NZ) for d in range...  34.9 us
    ppermute x7, starting transfers between devices, along_z(): lax.ppermute(v, 'space', [(d, d // NZ * NZ + (d + s) % NZ) for d in range...  25.8 us
    pallas_call x1, Pallas kernels, owner(): pl.pallas_call(owner_kernel, out_shape=jax.ShapeDtypeStruct((PAR, 128), B...  18.9 us
    pallas_call x1, Pallas kernels, unpack(): pl.pallas_call(unpack_kernel, out_shape=jax.ShapeDtypeStruct((rows, 128),...  9.11 us
    ppermute x3, starting transfers between devices, along_y(): return lax.ppermute(v, 'space', [(d, (d + i * NZ) % NS) for d in range(NS)])  6.81 us
  transfers between devices with their start and end apart: 10, of which 2 were waited for; matrix products, arithmetic and copies ran while one was open for 0% of the time, Pallas kernels for 41%

profile of v1, /device:TPU:2, one launch (start us, length us, event | category | flops | bytes accessed | tf_op | source)
XLA Modules:
  0.0 312.8 jit_solution(13522262372005748624)
XLA Ops:
  0.6 6.2 %pack.1 = (bf16[32,528,128]{2,1,0:T(8,128)(2,1)}, s32[32,8,128]{2,1,0:T(8,128)}, s32[32,8,128]{2,1,0:T(8,128)}, s32[32]{0:T(128)}, s32[32]{0:T(128)}, /*index=5*/s32[32]{0:T(128)}) custom-call(s32[64,128]{1,0:T(8,128)} %bitcast.22, s32[64,128]{1,0:T(8,128)} %bitcast.23, bf16[8192,128]{1,0:T(8,128)(2,1)} %bitcast.17), custom_call_target="tpu_custom_call" | custom-call | bytes 28800000 | tf_op jit(solution)/shard_map/pack/pallas_call | solution.py:83
  6.9 66.0 %exchange.1 = (bf16[8,2048,128]{2,1,0:T(8,128)(2,1)}, s32[32,8,128]{2,1,0:T(8,128)}, s32[32,8,128]{2,1,0:T(8,128)}, bf16[4,528,128]{2,1,0:T(8,128)(2,1)}, bf16[4...) custom-call(bf16[2048,128]{1,0:T(8,128)(2,1)} %bitcast.19, ...), custom_call_target="tpu_custom_call" | custom-call | bytes 180000000 | tf_op jit(solution)/shard_map/exchange/pallas_call | solution.py:220
  72.9 24.0 %proxy.2 = (bf16[8,528,128]{2,1,0:T(8,128)(2,1)}, bf16[8,528,128]{2,1,0:T(8,128)(2,1)}, f32[1024,128]{1,0:T(8,128)}) custom-call(s32[32768]{0:T(1024)} %bitcast.14, s32[32,8,128]{2,1,0:T(8,128)} %get-tuple-element.35.refs_1_, bf16[16384,128]{1,0:T(8,128)(2,1)} %bitcast.11, bf16[8,128,128]{2,1,0:T(8,128)(2,1)} %refs_3_.3, ...), custom_call_target="tpu_custom_call" | custom-call | bytes 72000000 | tf_op jit(solution)/shard_map/proxy/pallas_call | solution.py:310
  96.9 2.4 collective-permute-start
  99.3 2.3 collective-permute-start.1
  101.6 24.2 %proxy.3 = (bf16[8,528,128]{2,1,0:T(8,128)(2,1)}, bf16[8,528,128]{2,1,0:T(8,128)(2,1)}, f32[1024,128]{1,0:T(8,128)}) custom-call(s32[32768]{0:T(1024)} %bitcast.15, s32[32,8,128]{2,1,0:T(8,128)} %get-tuple-element.35.refs_1_, bf16[16384,128]{1,0:T(8,128)(2,1)} %bitcast.12, bf16[8,128,128]{2,1,0:T(8,128)(2,1)} %refs_3_.3, ...), custom_call_target="tpu_custom_call" | custom-call | bytes 72000000 | tf_op jit(solution)/shard_map/proxy/pallas_call | solution.py:310
  125.8 2.1 collective-permute-start.2
  127.9 1.4 collective-permute-start.3
  129.4 1.8 collective-permute-start.4
  131.1 15.3 %collective-permute-done.3.rest_1_ = bf16[4,528,128]{2,1,0:T(8,128)(2,1)S(1)} collective-permute-done((bf16[4,528,128]{2,1,0:T(8,128)(2,1)S(1)}, bf16[4,528,128]{2,1,0:T(8,128)(2,1)S(1)}, u32[]{:S(2)}, u32[]{:S(2)}) %collective-permute-start.3) | collective-permute-done | bytes 540704 | tf_op jit(solution)/shard_map/ppermute | solution.py:525
  146.5 6.2 %collective-permute-start.5 = (bf16[4,528,128]{2,1,0:T(8,128)(2,1)S(1)}, bf16[4,528,128]{2,1,0:T(8,128)(2,1)S(1)}, u32[]{:S(2)}, u32[]{:S(2)}) collective-permute-start(bf16[4,528,128]{2,1,0:T(8,128)(2,1)S(1)} %copy-done.4), channel_id=1, source_target_pairs={{0,3},{1,4},{2,5},{3,6},{4,7},{5,0},{6,1},{7,2},{8,11},{9,12},{10,... | collective-permute-start | bytes 1622024 | tf_op jit(solution)/shard_map/ppermute | solution.py:525
  152.6 19.5 %collective-permute-done.4.rest_2_ = bf16[4,528,128]{2,1,0:T(8,128)(2,1)S(1)} collective-permute-done((bf16[4,528,128]{2,1,0:T(8,128)(2,1)S(1)}, bf16[4,528,128]{2,1,0:T(8,128)(2,1)S(1)}, u32[]{:S(2)}, u32[]{:S(2)}) %collective-permute-start.4) | collective-permute-done | bytes 540704 | tf_op jit(solution)/shard_map/ppermute | solution.py:525
  172.2 8.5 %collective-permute-start.6 = (bf16[4,528,128]{2,1,0:T(8,128)(2,1)S(1)}, bf16[4,528,128]{2,1,0:T(8,128)(2,1)}, u32[]{:S(2)}, u32[]{:S(2)}) collective-permute-start(bf16[4,528,128]{2,1,0:T(8,128)(2,1)S(1)} %copy-done.3), channel_id=1, source_target_pairs={{0,4},{1,5},{2,6},{3,7},{4,0},{5,1},{6,2},{7,3},{8,12},{9,13},{10,... | collective-permute-start | bytes 1622024 | tf_op jit(solution)/shard_map/ppermute | solution.py:525
  180.7 0.0 collective-permute-done.b1
  180.7 0.0 collective-permute-done.1.b2
  180.7 1.6 collective-permute-start.8
  182.3 0.0 collective-permute-done.2.b3
  182.3 6.4 %collective-permute-start.9 = (bf16[4,528,128]{2,1,0:T(8,128)(2,1)S(1)}, bf16[4,528,128]{2,1,0:T(8,128)(2,1)}, u32[]{:S(2)}, u32[]{:S(2)}) collective-permute-start(bf16[4,528,128]{2,1,0:T(8,128)(2,1)S(1)} %copy-done), channel_id=1, source_target_pairs={{0,7},{1,0},{2,1},{3,2},{4,3},{5,4},{6,5},{7,6},{8,15},{9,8},{10,9... | collective-permute-start | bytes 1622024 | tf_op jit(solution)/shard_map/ppermute | solution.py:525
  188.7 94.4 %total.1 = f32[1024,128]{1,0:T(8,128)} custom-call(f32[1024,128]{1,0:T(8,128)} %get-tuple-element.45.refs_0_, f32[1024,128]{1,0:T(8,128)} %get-tuple-element.46.refs_1_), custom_call_target="tpu_custom_call" | custom-call | bytes 118800000 | tf_op jit(solution)/shard_map/total/pallas_call | solution.py:448
  283.1 9.1 %unpack.1 = bf16[8192,128]{1,0:T(8,128)(2,1)} custom-call(s32[32]{0:T(128)} %get-tuple-element.47.first_ref, s32[32]{0:T(128)} %get-tuple-element.48.lo_ref, s32[32]{0:T(128)} %get-tuple-element.49.hi_ref, bf16[8,528,128]{2,1,0:T(8,128)(2,1)} %get-tuple-element.50.b0, bf16[8,528,128]{2,1,0:T(8,128)(2,1)} %collective-permute-done.b1, ...), custom_call_target="tpu_custom_call" | custom-call | bytes 28800000 | tf_op jit(solution)/shard_map/unpack/pallas_call | solution.py:504
  292.2 0.0 collective-permute-done.5.rest_3_
  292.2 0.8 copy-done.11
  293.0 18.9 %owner.1 = bf16[2048,128]{1,0:T(8,128)(2,1)} custom-call(s32[32768]{0:T(1024)} %bitcast.21, bf16[1024,128]{1,0:T(8,128)(2,1)} %bitcast.13, bf16[4,528,128]{2,1,0:T(8,128)(2,1)} %get-tuple-element.37.refs_4_.rest_0_, bf16[4,528,128]{2,1,0:T(8,128)(2,1)} %copy-done.9, bf16[4,528,128]{2,1,0:T(8,128)(2,1)} %copy-done.10, bf16[4,528,128]{2,1,0:T(8,128)(2,1)} %copy-done.11, ...), custom_call_target="tpu_custom_call" | custom-call | bytes 64800000 | tf_op jit(solution)/shard_map/owner/pallas_call | solution.py:377
  312.0 0.8 copy.9
  (28 shorter events, 0.1 us)
Async XLA Ops:
  96.9 83.8 %collective-permute-start = (bf16[8,528,128]{2,1,0:T(8,128)(2,1)}, bf16[8,528,128]{2,1,0:T(8,128)(2,1)}, u32[]{:S(2)}, u32[]{:S(2)}) collective-permute-start(bf16[8,528,128]{2,1,0:T(8,128)(2,1)} %get-tuple-element.51), channel_id=1, source_target_pairs={{0,8},{1,9},{2,10},{3,11},{4,12},{5,13},{6,14},{7,15},{8,16},{9,17... | collective-permute-start | bytes 3244040 | tf_op jit(solution)/shard_map/ppermute | solution.py:530
  99.3 28.6 %copy-start.6 = (bf16[4,528,128]{2,1,0:T(8,128)(2,1)S(1)}, bf16[4,528,128]{2,1,0:T(8,128)(2,1)}, u32[]{:S(2)}) copy-start(bf16[4,528,128]{2,1,0:T(8,128)(2,1)} %get-tuple-element.38.refs_5_) | copy-start | bytes 1622020
  99.3 30.1 %copy-start.5 = (bf16[4,528,128]{2,1,0:T(8,128)(2,1)S(1)}, bf16[4,528,128]{2,1,0:T(8,128)(2,1)}, u32[]{:S(2)}) copy-start(bf16[4,528,128]{2,1,0:T(8,128)(2,1)} %get-tuple-element.39.refs_6_) | copy-start | bytes 1622020
  99.3 47.2 %copy-start.4 = (bf16[4,528,128]{2,1,0:T(8,128)(2,1)S(1)}, bf16[4,528,128]{2,1,0:T(8,128)(2,1)}, u32[]{:S(2)}) copy-start(bf16[4,528,128]{2,1,0:T(8,128)(2,1)} %get-tuple-element.40.refs_7_) | copy-start | bytes 1622020
  99.3 72.9 %copy-start.3 = (bf16[4,528,128]{2,1,0:T(8,128)(2,1)S(1)}, bf16[4,528,128]{2,1,0:T(8,128)(2,1)}, u32[]{:S(2)}) copy-start(bf16[4,528,128]{2,1,0:T(8,128)(2,1)} %get-tuple-element.41.refs_8_) | copy-start | bytes 1622020
  99.3 81.4 %copy-start.2 = (bf16[4,528,128]{2,1,0:T(8,128)(2,1)S(1)}, bf16[4,528,128]{2,1,0:T(8,128)(2,1)}, u32[]{:S(2)}) copy-start(bf16[4,528,128]{2,1,0:T(8,128)(2,1)} %get-tuple-element.42.refs_9_) | copy-start | bytes 1622020
  99.3 81.4 %copy-start.1 = (bf16[4,528,128]{2,1,0:T(8,128)(2,1)S(1)}, bf16[4,528,128]{2,1,0:T(8,128)(2,1)}, u32[]{:S(2)}) copy-start(bf16[4,528,128]{2,1,0:T(8,128)(2,1)} %get-tuple-element.43.refs_10_) | copy-start | bytes 1622020
  99.3 83.0 %copy-start = (bf16[4,528,128]{2,1,0:T(8,128)(2,1)S(1)}, bf16[4,528,128]{2,1,0:T(8,128)(2,1)}, u32[]{:S(2)}) copy-start(bf16[4,528,128]{2,1,0:T(8,128)(2,1)} %get-tuple-element.44.refs_11_) | copy-start | bytes 1622020
  99.3 81.3 %collective-permute-start.1 = (bf16[8,528,128]{2,1,0:T(8,128)(2,1)}, bf16[8,528,128]{2,1,0:T(8,128)(2,1)}, u32[]{:S(2)}, u32[]{:S(2)}) collective-permute-start(bf16[8,528,128]{2,1,0:T(8,128)(2,1)} %get-tuple-element.52), channel_id=1, source_target_pairs={{0,16},{1,17},{2,18},{3,19},{4,20},{5,21},{6,22},{7,23},{8,24},{9,... | collective-permute-start | bytes 3244040 | tf_op jit(solution)/shard_map/ppermute | solution.py:530
  125.8 56.5 %collective-permute-start.2 = (bf16[8,528,128]{2,1,0:T(8,128)(2,1)}, bf16[8,528,128]{2,1,0:T(8,128)(2,1)S(1)}, u32[]{:S(2)}, u32[]{:S(2)}) collective-permute-start(bf16[8,528,128]{2,1,0:T(8,128)(2,1)} %get-tuple-element.53), channel_id=1, source_target_pairs={{0,24},{1,25},{2,26},{3,27},{4,28},{5,29},{6,30},{7,31},{8,0},{9,1... | collective-permute-start | bytes 3244040 | tf_op jit(solution)/shard_map/ppermute | solution.py:530
  127.9 18.5 %collective-permute-start.3 = (bf16[4,528,128]{2,1,0:T(8,128)(2,1)S(1)}, bf16[4,528,128]{2,1,0:T(8,128)(2,1)S(1)}, u32[]{:S(2)}, u32[]{:S(2)}) collective-permute-start(bf16[4,528,128]{2,1,0:T(8,128)(2,1)S(1)} %copy-done.6), channel_id=1, source_target_pairs={{0,1},{1,2},{2,3},{3,4},{4,5},{5,6},{6,7},{7,0},{8,9},{9,10},{10,1... | collective-permute-start | bytes 1622024 | tf_op jit(solution)/shard_map/ppermute | solution.py:525
  129.4 42.8 %collective-permute-start.4 = (bf16[4,528,128]{2,1,0:T(8,128)(2,1)S(1)}, bf16[4,528,128]{2,1,0:T(8,128)(2,1)S(1)}, u32[]{:S(2)}, u32[]{:S(2)}) collective-permute-start(bf16[4,528,128]{2,1,0:T(8,128)(2,1)S(1)} %copy-done.5), channel_id=1, source_target_pairs={{0,2},{1,3},{2,4},{3,5},{4,6},{5,7},{6,0},{7,1},{8,10},{9,11},{10,... | collective-permute-start | bytes 1622024 | tf_op jit(solution)/shard_map/ppermute | solution.py:525
  146.5 42.2 %copy-start.9 = (bf16[4,528,128]{2,1,0:T(8,128)(2,1)}, bf16[4,528,128]{2,1,0:T(8,128)(2,1)S(1)}, u32[]{:S(2)}) copy-start(bf16[4,528,128]{2,1,0:T(8,128)(2,1)S(1)} %collective-permute-done.3.rest_1_) | copy-start | bytes 1622020
  146.5 145.7 %collective-permute-start.5 = (bf16[4,528,128]{2,1,0:T(8,128)(2,1)S(1)}, bf16[4,528,128]{2,1,0:T(8,128)(2,1)S(1)}, u32[]{:S(2)}, u32[]{:S(2)}) collective-permute-start(bf16[4,528,128]{2,1,0:T(8,128)(2,1)S(1)} %copy-done.4), channel_id=1, source_target_pairs={{0,3},{1,4},{2,5},{3,6},{4,7},{5,0},{6,1},{7,2},{8,11},{9,12},{10,... | collective-permute-start | bytes 1622024 | tf_op jit(solution)/shard_map/ppermute | solution.py:525
  172.2 16.5 %copy-start.10 = (bf16[4,528,128]{2,1,0:T(8,128)(2,1)}, bf16[4,528,128]{2,1,0:T(8,128)(2,1)S(1)}, u32[]{:S(2)}) copy-start(bf16[4,528,128]{2,1,0:T(8,128)(2,1)S(1)} %collective-permute-done.4.rest_2_) | copy-start | bytes 1622020
  172.2 120.0 %collective-permute-start.6 = (bf16[4,528,128]{2,1,0:T(8,128)(2,1)S(1)}, bf16[4,528,128]{2,1,0:T(8,128)(2,1)}, u32[]{:S(2)}, u32[]{:S(2)}) collective-permute-start(bf16[4,528,128]{2,1,0:T(8,128)(2,1)S(1)} %copy-done.3), channel_id=1, source_target_pairs={{0,4},{1,5},{2,6},{3,7},{4,0},{5,1},{6,2},{7,3},{8,12},{9,13},{10,... | collective-permute-start | bytes 1622024 | tf_op jit(solution)/shard_map/ppermute | solution.py:525
  180.7 111.5 %collective-permute-start.7 = (bf16[4,528,128]{2,1,0:T(8,128)(2,1)S(1)}, bf16[4,528,128]{2,1,0:T(8,128)(2,1)}, u32[]{:S(2)}, u32[]{:S(2)}) collective-permute-start(bf16[4,528,128]{2,1,0:T(8,128)(2,1)S(1)} %copy-done.2), channel_id=1, source_target_pairs={{0,5},{1,6},{2,7},{3,0},{4,1},{5,2},{6,3},{7,4},{8,13},{9,14},{10,... | collective-permute-start | bytes 1622024 | tf_op jit(solution)/shard_map/ppermute | solution.py:525
  180.7 111.5 %collective-permute-start.8 = (bf16[4,528,128]{2,1,0:T(8,128)(2,1)S(1)}, bf16[4,528,128]{2,1,0:T(8,128)(2,1)}, u32[]{:S(2)}, u32[]{:S(2)}) collective-permute-start(bf16[4,528,128]{2,1,0:T(8,128)(2,1)S(1)} %copy-done.1), channel_id=1, source_target_pairs={{0,6},{1,7},{2,0},{3,1},{4,2},{5,3},{6,4},{7,5},{8,14},{9,15},{10,... | collective-permute-start | bytes 1622024 | tf_op jit(solution)/shard_map/ppermute | solution.py:525
  182.3 6.4 %copy-start.8 = (bf16[8,528,128]{2,1,0:T(8,128)(2,1)}, bf16[8,528,128]{2,1,0:T(8,128)(2,1)S(1)}, u32[]{:S(2)}) copy-start(bf16[8,528,128]{2,1,0:T(8,128)(2,1)S(1)} %collective-permute-done.2.b3) | copy-start | bytes 3244036
  182.3 109.9 %collective-permute-start.9 = (bf16[4,528,128]{2,1,0:T(8,128)(2,1)S(1)}, bf16[4,528,128]{2,1,0:T(8,128)(2,1)}, u32[]{:S(2)}, u32[]{:S(2)}) collective-permute-start(bf16[4,528,128]{2,1,0:T(8,128)(2,1)S(1)} %copy-done), channel_id=1, source_target_pairs={{0,7},{1,0},{2,1},{3,2},{4,3},{5,4},{6,5},{7,6},{8,15},{9,8},{10,9... | collective-permute-start | bytes 1622024 | tf_op jit(solution)/shard_map/ppermute | solution.py:525
  292.2 0.9 copy-start.11
  293.0 18.9 %copy-start.7 = (f32[1024,128]{1,0:T(8,128)S(1)}, f32[1024,128]{1,0:T(8,128)}, u32[]{:S(2)}) copy-start(f32[1024,128]{1,0:T(8,128)} %total.1) | copy-start | bytes 1572868

commit v2 on v1

--- a/solution.py
+++ b/solution.py
@@ -105,8 +105,8 @@
     )(parents, codes, feats)
 
 
-def exchange_kernel(grad_ref, rows_ref, slots_ref, blk_ref, table_ref, want_ref, got_ref, *rest):
-    parts, (mine, ss, rs, ys, yr, gs, gr, fs, fr, local, stage) = rest[:NZ], rest[NZ:]
+def exchange_kernel(grad_ref, rows_ref, slots_ref, blk_ref, table_ref, want_ref, got_ref, near_ref, *rest):
+    parts, (ss, rs, ys, yr, gs, gr, fs, fr, ns, nr, local) = rest[:NZ], rest[NZ:]
     dp, me = lax.axis_index("dp"), lax.axis_index("space")
     y, z = me // NZ, lax.rem(me, NZ)
     barrier = pltpu.get_barrier_semaphore()
@@ -121,9 +121,7 @@
         pltpu.make_async_copy(rows_ref.at[pl.ds(y * NZ, NZ)], want_ref.at[pl.ds(y * NZ, NZ)], local.at[1]),
         pltpu.make_async_copy(slots_ref.at[me], got_ref.at[me], local.at[2]),
     ]
-    loads = [pltpu.make_async_copy(blk_ref.at[y * NZ + lax.rem(z + r, NZ)], mine.at[r], stage.at[r]) for r in range(NZ)]
-    stores = [pltpu.make_async_copy(mine.at[r], parts[r].at[y], local.at[3 + r]) for r in range(NZ)]
-    for copy in own + loads:
+    for copy in own:
         copy.start()
     pl.semaphore_wait(barrier, NS - 1)
     half = PAR // 2
@@ -160,7 +158,7 @@
         ty = lax.rem(y + i, NY)
         return pltpu.make_async_remote_copy(
             blk_ref.at[ty * NZ + lax.rem(z + r, NZ)],
-            parts[r].at[y],
+            parts[r].at[i - 1],
             fs.at[i, r],
             fr.at[i, r],
             device_id=(dp, ty * NZ + z),
@@ -168,6 +166,19 @@
         )
 
     moves = [block_to(i, r) for r in range(NZ) for i in range(1, NY)]
+
+    def straight(r):
+        tz = lax.rem(z + r, NZ)
+        return pltpu.make_async_remote_copy(
+            blk_ref.at[y * NZ + tz],
+            near_ref.at[r],
+            ns.at[r],
+            nr.at[r],
+            device_id=(dp, y * NZ + tz),
+            device_id_type=MESH,
+        )
+
+    straights = [straight(r) for r in (1, 7, 2, 6, 3, 5, 4)]
 
     def slots_to(i):
         t = lax.rem(me + i, NS)
@@ -188,17 +199,17 @@
     lax.fori_loop(1, NS, start_slots, 0)
     for move in moves:
         move.start()
-    for load, put in zip(loads, stores):
-        load.wait()
-        put.start()
     for k, i in chain:
+        if (k, i) == (2, 1):
+            for move in straights:
+                move.start()
         for side in range(2):
             hops[k, side, i].wait_recv()
             if (k + 1, side, i) in hops:
                 hops[k + 1, side, i].start()
     for copy in hops.values():
         copy.wait_send()
-    for move in moves:
+    for move in moves + straights:
         move.wait()
     for i in range(1, NY):
         rows_to(i).wait()
@@ -208,26 +219,27 @@
         return c
 
     lax.fori_loop(1, NS, end_slots, 0)
-    for copy in own + stores:
+    for copy in own:
         copy.wait()
 
 
 def exchange(grad, rows, slots, blocks):
     ints = jax.ShapeDtypeStruct((NS, 8, 128), I32)
-    part = jax.ShapeDtypeStruct((NY, CAP, 128), BF16)
+    part = jax.ShapeDtypeStruct((NY - 1, CAP, 128), BF16)
+    near = jax.ShapeDtypeStruct((NZ, CAP, 128), BF16)
     dma = pltpu.SemaphoreType.DMA
-    sems = [(2, 4, 2), (2, 4, 2), (NY,), (NY,), (NS,), (NS,), (NY, NZ), (NY, NZ), (3 + NZ,), (NZ,)]
+    sems = [(2, 4, 2), (2, 4, 2), (NY,), (NY,), (NS,), (NS,), (NY, NZ), (NY, NZ), (NZ,), (NZ,), (3,)]
     out = pl.pallas_call(
         exchange_kernel,
-        out_shape=(jax.ShapeDtypeStruct((NZ, PAR, 128), BF16), ints, ints) + (part,) * NZ,
-        in_specs=[VM] + [ANY] * 3,
-        out_specs=(VM,) + (ANY,) * (2 + NZ),
-        scratch_shapes=[pltpu.VMEM((NZ, CAP, 128), BF16)] + [dma(n) for n in sems],
-        compiler_params=pltpu.CompilerParams(collective_id=1, has_side_effects=True, vmem_limit_bytes=VLIM),
+        out_shape=(jax.ShapeDtypeStruct((NZ, PAR, 128), BF16), ints, ints, near) + (part,) * NZ,
+        in_specs=[ANY] * 4,
+        out_specs=(ANY,) * (4 + NZ),
+        scratch_shapes=[dma(n) for n in sems],
+        compiler_params=pltpu.CompilerParams(collective_id=1, has_side_effects=True),
         cost_estimate=cost(50),
         name="exchange",
     )(grad, rows, slots, blocks)
-    return out[0], out[1], out[2], out[3:]
+    return *out[:4], out[4:]
 
 
 def place():
@@ -235,13 +247,15 @@
     return me >> 3, me & (NZ - 1)
 
 
-def proxy_kernel(distances, want_ref, codes_ref, table_ref, weight_ref, *rest):
+def proxy_kernel(distances, want_ref, codes_ref, table_ref, weight_ref, blk_ref, *rest):
     n = len(distances)
     parts, outs = rest[:NZ], rest[NZ : NZ + n]
     term_ref, wide, rowbuf, feats, acc, turned_weight, sems = rest[NZ + n :]
     y, z = place()
     copies = [
-        pltpu.make_async_copy(part.at[(y + i) & (NY - 1)], feats.at[r, m], sems.at[r, m])
+        pltpu.make_async_copy(
+            part.at[NY - 1 - i] if i else blk_ref.at[y * NZ + ((z + r) & (NZ - 1))], feats.at[r, m], sems.at[r, m]
+        )
         for m, i in enumerate(distances)
         for r, part in enumerate(parts)
     ]
@@ -305,13 +319,13 @@
         term_ref[part, :] = acc[:, part]
 
 
-def proxy(distances, want, table, weight, parts):
+def proxy(distances, want, table, weight, blocks, parts):
     n = len(distances)
     *rows, term = pl.pallas_call(
         lambda *refs: proxy_kernel(distances, *refs),
         out_shape=(jax.ShapeDtypeStruct((NZ, CAP, 128), BF16),) * n
         + (jax.ShapeDtypeStruct((KINDS * 128, 128), F32),),
-        in_specs=[SM, VM, VM, VM] + [ANY] * NZ,
+        in_specs=[SM, VM, VM, VM] + [ANY] * (NZ + 1),
         out_specs=(VM,) * (n + 1),
         scratch_shapes=[
             pltpu.VMEM((NZ * PAR, 128), F32),
@@ -324,17 +338,24 @@
         compiler_params=pltpu.CompilerParams(vmem_limit_bytes=VLIM),
         cost_estimate=cost(20),
         name="proxy",
-    )(want.reshape(-1), want, table, weight, *parts)
+    )(want.reshape(-1), want, table, weight, blocks, *parts)
     return dict(zip(distances, rows)), term
 
 
-def owner_kernel(slot_ref, weight_ref, *rest):
+def owner_kernel(slot_ref, weight_ref, blk_ref, near_ref, *rest):
     parts = rest[:NZ]
     out_ref, grid_ref, rowbuf, feats, sems = rest[NZ:]
-    _, z = place()
-    copies = [pltpu.make_async_copy(part, feats.at[s], sems.at[s]) for s, part in enumerate(parts)]
-    for copy in copies:
-        copy.start()
+    y, z = place()
+    copies = [
+        (
+            pltpu.make_async_copy(part, feats.at[s, pl.ds(1, NY - 1)], sems.at[s, 0]),
+            pltpu.make_async_copy(near_ref.at[s] if s else blk_ref.at[y * NZ + z], feats.at[s, 0], sems.at[s, 1]),
+        )
+        for s, part in enumerate(parts)
+    ]
+    for pair in copies:
+        for copy in pair:
+            copy.start()
 
     def clear(i, c):
         grid_ref[pl.ds(pl.multiple_of(i * 512, 512), 512), :] = jnp.zeros((512, 128), F32)
@@ -343,12 +364,13 @@
     lax.fori_loop(0, SLOTS // 512, clear, 0)
 
     for s in range(NZ):
-        copies[s].wait()
-
-        def block(q, c, s=s):
-            base = (q * NZ + ((z - s) & (NZ - 1))) * 1024
+        for copy in copies[s]:
+            copy.wait()
+
+        def block(i, c, s=s):
+            base = (((y - i) & (NY - 1)) * NZ + ((z - s) & (NZ - 1))) * 1024
             lo, hi = slot_ref[base + 1022], slot_ref[base + 1023]
-            rowbuf[...] = feats[s, q].astype(F32)
+            rowbuf[...] = feats[s, i].astype(F32)
 
             def group(g, c):
                 for u in range(16):
@@ -373,22 +395,22 @@
     lax.fori_loop(0, PAR // 512, chunk, 0)
 
 
-def owner(slots, weight, parts):
+def owner(slots, weight, blocks, near, parts):
     return pl.pallas_call(
         owner_kernel,
         out_shape=jax.ShapeDtypeStruct((PAR, 128), BF16),
-        in_specs=[SM, VM] + [ANY] * NZ,
+        in_specs=[SM, VM] + [ANY] * (NZ + 2),
         out_specs=VM,
         scratch_shapes=[
             pltpu.VMEM((SLOTS + 8, 128), F32),
             pltpu.VMEM((CAP, 128), F32),
             pltpu.VMEM((NZ, NY, CAP, 128), BF16),
-            pltpu.SemaphoreType.DMA((NZ,)),
+            pltpu.SemaphoreType.DMA((NZ, 2)),
         ],
         compiler_params=pltpu.CompilerParams(vmem_limit_bytes=VLIM),
         cost_estimate=cost(18),
         name="owner",
-    )(slots.reshape(-1), weight, *parts)
+    )(slots.reshape(-1), weight, blocks, near, *parts)
 
 
 def total_kernel(scale, far_ref, near_ref, out_ref, term_ref, b1, s1, b2, s2, b3, s3, b4, s4, send, recv):
@@ -517,7 +539,7 @@
     fine_rows = feats.shape[0]
     as2d = lambda v: v.reshape(fine_rows // 128, 128)
     blocks, slots, rows, first, lo, hi = pack(as2d(child_parent[0]), as2d(child_code[0]), feats)
-    table, want, got, parts = exchange(cotangent, rows, slots, blocks)
+    table, want, got, near_blocks, parts = exchange(cotangent, rows, slots, blocks)
 
     def along_z(v, s):
         if s == 0:
@@ -531,8 +553,8 @@
 
     arrived = [along_z(v, s) for s, v in enumerate(parts)]
     table = table.reshape(NZ * PAR, 128)
-    far, far_term = proxy((2, 1), want, table, weight, parts)
-    near, near_term = proxy((3, 0), want, table, weight, parts)
+    far, far_term = proxy((2, 1), want, table, weight, blocks, parts)
+    near, near_term = proxy((3, 0), want, table, weight, blocks, parts)
     reply = {**far, **near}
     back = [along_y(reply[i], i) for i in range(NY)]
     grad_rows = fine_rows * NS * lax.axis_size("dp")
@@ -540,7 +562,7 @@
     first, weight_grad = lax.optimization_barrier((first, weight_grad))
     feature_grad = unpack(first, lo, hi, back, fine_rows)
     got, feature_grad = lax.optimization_barrier((got, feature_grad))
-    result = owner(got, weight.reshape(KINDS * 128, 128), arrived)
+    result = owner(got, weight.reshape(KINDS * 128, 128), blocks, near_blocks, arrived)
     return result[None], feature_grad[None], weight_grad.reshape(KINDS, 128, 128)
 
 

time: 318 us -> 295 us (0.928)
  Pallas kernels: 243 us -> 230 us
  starting transfers between devices: 32.6 us -> 22.5 us
    pallas_call x1, Pallas kernels: 94.4 us -> 70 us  [total(): pl.pallas_call(lambda *refs: total_kernel(scale, *refs), out_shape=jax.Sh...]
    pallas_call x1, Pallas kernels: 66 us -> 77.3 us  [exchange(): pl.pallas_call(exchange_kernel, out_shape=(jax.ShapeDtypeStruct((NZ, PAR,...]
    ppermute x7, starting transfers between devices: 25.8 us -> 15.5 us  [along_z(): lax.ppermute(v, 'space', [(d, d // NZ * NZ + (d + s) % NZ) for d in range...]
  transfers between devices with their start and end apart: 10 -> 10, of which waited for: 2 -> 2; matrix products, arithmetic and copies ran while one was open for 0% -> 0% of each run, Pallas kernels for 41% -> 35%
where the time goes in v2:
time: 295 us; the launch traced here: 292 us
  Pallas kernels  230 us (78%)
  waiting for transfers between devices  36.9 us (13%)
  starting transfers between devices  22.5 us (8%)
    pallas_call x1, Pallas kernels, exchange(): pl.pallas_call(exchange_kernel, out_shape=(jax.ShapeDtypeStruct((NZ, PAR,...  77.3 us
    pallas_call x1, Pallas kernels, total(): pl.pallas_call(lambda *refs: total_kernel(scale, *refs), out_shape=jax.Sh...  70 us
    pallas_call x2, Pallas kernels, proxy(): pl.pallas_call(lambda *refs: proxy_kernel(distances, *refs), out_shape=(j...  48.2 us
    ppermute x7, waiting for transfers between devices, along_z(): lax.ppermute(v, 'space', [(d, d // NZ * NZ + (d + s) % NZ) for d in range...  36.9 us
    pallas_call x1, Pallas kernels, owner(): pl.pallas_call(owner_kernel, out_shape=jax.ShapeDtypeStruct((PAR, 128), B...  19 us
    ppermute x7, starting transfers between devices, along_z(): lax.ppermute(v, 'space', [(d, d // NZ * NZ + (d + s) % NZ) for d in range...  15.5 us
    pallas_call x1, Pallas kernels, unpack(): pl.pallas_call(unpack_kernel, out_shape=jax.ShapeDtypeStruct((rows, 128),...  9.11 us
    ppermute x3, starting transfers between devices, along_y(): return lax.ppermute(v, 'space', [(d, (d + i * NZ) % NS) for d in range(NS)])  6.97 us
  transfers between devices with their start and end apart: 10, of which 2 were waited for; matrix products, arithmetic and copies ran while one was open for 0% of the time, Pallas kernels for 35%

profile of v2, /device:TPU:2, one launch (start us, length us, event | category | flops | bytes accessed | tf_op | source)
XLA Modules:
  0.0 291.5 jit_solution(5998330830664746854)
XLA Ops:
  0.6 6.2 %pack.1 = (bf16[32,528,128]{2,1,0:T(8,128)(2,1)}, s32[32,8,128]{2,1,0:T(8,128)}, s32[32,8,128]{2,1,0:T(8,128)}, s32[32]{0:T(128)}, s32[32]{0:T(128)}, /*index=5*/s32[32]{0:T(128)}) custom-call(s32[64,128]{1,0:T(8,128)} %bitcast.22, s32[64,128]{1,0:T(8,128)} %bitcast.23, bf16[8192,128]{1,0:T(8,128)(2,1)} %bitcast.17), custom_call_target="tpu_custom_call" | custom-call | bytes 28800000 | tf_op jit(solution)/shard_map/pack/pallas_call | solution.py:83
  6.9 77.3 %exchange.1 = (bf16[8,2048,128]{2,1,0:T(8,128)(2,1)}, s32[32,8,128]{2,1,0:T(8,128)}, s32[32,8,128]{2,1,0:T(8,128)}, bf16[8,528,128]{2,1,0:T(8,128)(2,1)}, bf16[3...) custom-call(bf16[2048,128]{1,0:T(8,128)(2,1)} %bitcast.19, ...), custom_call_target="tpu_custom_call" | custom-call | bytes 180000000 | tf_op jit(solution)/shard_map/exchange/pallas_call | solution.py:232
  84.1 24.2 %proxy.3 = (bf16[8,528,128]{2,1,0:T(8,128)(2,1)}, bf16[8,528,128]{2,1,0:T(8,128)(2,1)}, f32[1024,128]{1,0:T(8,128)}) custom-call(s32[32768]{0:T(1024)} %bitcast.14, s32[32,8,128]{2,1,0:T(8,128)} %get-tuple-element.36.refs_1_, bf16[16384,128]{1,0:T(8,128)(2,1)} %bitcast.11, bf16[8,128,128]{2,1,0:T(8,128)(2,1)} %refs_3_.3, ...), custom_call_target="tpu_custom_call" | custom-call | bytes 72000000 | tf_op jit(solution)/shard_map/proxy/pallas_call | solution.py:324
  108.4 2.3 collective-permute-start.2
  110.7 24.0 %proxy.2 = (bf16[8,528,128]{2,1,0:T(8,128)(2,1)}, bf16[8,528,128]{2,1,0:T(8,128)(2,1)}, f32[1024,128]{1,0:T(8,128)}) custom-call(s32[32768]{0:T(1024)} %bitcast.15, s32[32,8,128]{2,1,0:T(8,128)} %get-tuple-element.36.refs_1_, bf16[16384,128]{1,0:T(8,128)(2,1)} %bitcast.12, bf16[8,128,128]{2,1,0:T(8,128)(2,1)} %refs_3_.3, ...), custom_call_target="tpu_custom_call" | custom-call | bytes 72000000 | tf_op jit(solution)/shard_map/proxy/pallas_call | solution.py:324
  134.7 2.3 collective-permute-start
  137.0 2.4 collective-permute-start.1
  139.3 3.7 %collective-permute-start.3 = (bf16[3,528,128]{2,1,0:T(8,128)(2,1)S(1)}, bf16[3,528,128]{2,1,0:T(8,128)(2,1)S(1)}, u32[]{:S(2)}, u32[]{:S(2)}) collective-permute-start(bf16[3,528,128]{2,1,0:T(8,128)(2,1)S(1)} %copy-done.7), channel_id=1, source_target_pairs={{0,1},{1,2},{2,3},{3,4},{4,5},{5,6},{6,7},{7,0},{8,9},{9,10},{10,1... | collective-permute-start | bytes 1216520 | tf_op jit(solution)/shard_map/ppermute | solution.py:547
  143.1 14.4 %collective-permute-done.3.rest_1_ = bf16[3,528,128]{2,1,0:T(8,128)(2,1)S(1)} collective-permute-done((bf16[3,528,128]{2,1,0:T(8,128)(2,1)S(1)}, bf16[3,528,128]{2,1,0:T(8,128)(2,1)S(1)}, u32[]{:S(2)}, u32[]{:S(2)}) %collective-permute-start.3) | collective-permute-done | bytes 405536 | tf_op jit(solution)/shard_map/ppermute | solution.py:547
  157.5 1.9 collective-permute-start.5
  159.4 22.5 %collective-permute-done.4.rest_2_ = bf16[3,528,128]{2,1,0:T(8,128)(2,1)S(1)} collective-permute-done((bf16[3,528,128]{2,1,0:T(8,128)(2,1)S(1)}, bf16[3,528,128]{2,1,0:T(8,128)(2,1)S(1)}, u32[]{:S(2)}, u32[]{:S(2)}) %collective-permute-start.4) | collective-permute-done | bytes 405536 | tf_op jit(solution)/shard_map/ppermute | solution.py:547
  181.9 0.0 collective-permute-start.6
  181.9 0.0 collective-permute-done.2.b3
  181.9 3.3 %collective-permute-start.7 = (bf16[3,528,128]{2,1,0:T(8,128)(2,1)S(1)}, bf16[3,528,128]{2,1,0:T(8,128)(2,1)}, u32[]{:S(2)}, u32[]{:S(2)}) collective-permute-start(bf16[3,528,128]{2,1,0:T(8,128)(2,1)S(1)} %copy-done.3), channel_id=1, source_target_pairs={{0,5},{1,6},{2,7},{3,0},{4,1},{5,2},{6,3},{7,4},{8,13},{9,14},{10,... | collective-permute-start | bytes 1216520 | tf_op jit(solution)/shard_map/ppermute | solution.py:547
  185.3 0.0 collective-permute-done.b1
  185.3 4.1 %collective-permute-start.8 = (bf16[3,528,128]{2,1,0:T(8,128)(2,1)S(1)}, bf16[3,528,128]{2,1,0:T(8,128)(2,1)}, u32[]{:S(2)}, u32[]{:S(2)}) collective-permute-start(bf16[3,528,128]{2,1,0:T(8,128)(2,1)S(1)} %copy-done.2), channel_id=1, source_target_pairs={{0,6},{1,7},{2,0},{3,1},{4,2},{5,3},{6,4},{7,5},{8,14},{9,15},{10,... | collective-permute-start | bytes 1216520 | tf_op jit(solution)/shard_map/ppermute | solution.py:547
  189.3 2.5 collective-permute-start.9
  191.8 70.0 %total.1 = f32[1024,128]{1,0:T(8,128)} custom-call(f32[1024,128]{1,0:T(8,128)} %get-tuple-element.46.refs_0_, f32[1024,128]{1,0:T(8,128)} %get-tuple-element.47.refs_1_), custom_call_target="tpu_custom_call" | custom-call | bytes 118800000 | tf_op jit(solution)/shard_map/total/pallas_call | solution.py:470
  261.8 9.1 %unpack.1 = bf16[8192,128]{1,0:T(8,128)(2,1)} custom-call(s32[32]{0:T(128)} %get-tuple-element.48.first_ref, s32[32]{0:T(128)} %get-tuple-element.49.lo_ref, s32[32]{0:T(128)} %get-tuple-element.50.hi_ref, bf16[8,528,128]{2,1,0:T(8,128)(2,1)} %get-tuple-element.51.b0, bf16[8,528,128]{2,1,0:T(8,128)(2,1)} %copy-done.9, bf16[8,528,128]{2,1,0:T(8,128)(2,1)} %copy-done.10, ...), custom_call_target="tpu_custom_call" | custom-call | bytes 28800000 | tf_op jit(solution)/shard_map/unpack/pallas_call | solution.py:526
  270.9 0.0 collective-permute-done.6.rest_4_
  271.0 0.0 collective-permute-done.7.rest_5_
  271.0 0.7 copy-done.13
  271.7 19.0 %owner.1 = bf16[2048,128]{1,0:T(8,128)(2,1)} custom-call(s32[32768]{0:T(1024)} %bitcast.21, bf16[1024,128]{1,0:T(8,128)(2,1)} %bitcast.13, bf16[32,528,128]{2,1,0:T(8,128)(2,1)} %get-tuple-element.33.blk_ref.refs_4_, bf16[8,528,128]{2,1,0:T(8,128)(2,1)} %get-tuple-element.56.near_ref, bf16[3,528,128]{2,1,0:T(8,128)(2,1)} %get-tuple-element.38.refs_5_.rest_0_, ...), custom_call_target="tpu_custom_call" | custom-call | bytes 64800000 | tf_op jit(solution)/shard_map/owner/pallas_call | solution.py:399
  290.7 0.8 copy.9
  (32 shorter events, 0.1 us)
Async XLA Ops:
  108.3 31.0 %copy-start.7 = (bf16[3,528,128]{2,1,0:T(8,128)(2,1)S(1)}, bf16[3,528,128]{2,1,0:T(8,128)(2,1)}, u32[]{:S(2)}) copy-start(bf16[3,528,128]{2,1,0:T(8,128)(2,1)} %get-tuple-element.39.refs_6_) | copy-start | bytes 1216516
  108.4 34.7 %copy-start.6 = (bf16[3,528,128]{2,1,0:T(8,128)(2,1)S(1)}, bf16[3,528,128]{2,1,0:T(8,128)(2,1)}, u32[]{:S(2)}) copy-start(bf16[3,528,128]{2,1,0:T(8,128)(2,1)} %get-tuple-element.40.refs_7_) | copy-start | bytes 1216516
  108.4 49.1 %copy-start.5 = (bf16[3,528,128]{2,1,0:T(8,128)(2,1)S(1)}, bf16[3,528,128]{2,1,0:T(8,128)(2,1)}, u32[]{:S(2)}) copy-start(bf16[3,528,128]{2,1,0:T(8,128)(2,1)} %get-tuple-element.41.refs_8_) | copy-start | bytes 1216516
  108.4 73.5 %copy-start.4 = (bf16[3,528,128]{2,1,0:T(8,128)(2,1)S(1)}, bf16[3,528,128]{2,1,0:T(8,128)(2,1)}, u32[]{:S(2)}) copy-start(bf16[3,528,128]{2,1,0:T(8,128)(2,1)} %get-tuple-element.42.refs_9_) | copy-start | bytes 1216516
  108.4 73.5 %copy-start.3 = (bf16[3,528,128]{2,1,0:T(8,128)(2,1)S(1)}, bf16[3,528,128]{2,1,0:T(8,128)(2,1)}, u32[]{:S(2)}) copy-start(bf16[3,528,128]{2,1,0:T(8,128)(2,1)} %get-tuple-element.43.refs_10_) | copy-start | bytes 1216516
  108.4 76.9 %copy-start.2 = (bf16[3,528,128]{2,1,0:T(8,128)(2,1)S(1)}, bf16[3,528,128]{2,1,0:T(8,128)(2,1)}, u32[]{:S(2)}) copy-start(bf16[3,528,128]{2,1,0:T(8,128)(2,1)} %get-tuple-element.44.refs_11_) | copy-start | bytes 1216516
  108.4 80.9 %copy-start.1 = (bf16[3,528,128]{2,1,0:T(8,128)(2,1)S(1)}, bf16[3,528,128]{2,1,0:T(8,128)(2,1)}, u32[]{:S(2)}) copy-start(bf16[3,528,128]{2,1,0:T(8,128)(2,1)} %get-tuple-element.45.refs_12_) | copy-start | bytes 1216516
  108.4 73.5 %collective-permute-start.2 = (bf16[8,528,128]{2,1,0:T(8,128)(2,1)}, bf16[8,528,128]{2,1,0:T(8,128)(2,1)S(1)}, u32[]{:S(2)}, u32[]{:S(2)}) collective-permute-start(bf16[8,528,128]{2,1,0:T(8,128)(2,1)} %get-tuple-element.54), channel_id=1, source_target_pairs={{0,24},{1,25},{2,26},{3,27},{4,28},{5,29},{6,30},{7,31},{8,0},{9,1... | collective-permute-start | bytes 3244040 | tf_op jit(solution)/shard_map/ppermute | solution.py:552
  134.7 50.6 %collective-permute-start = (bf16[8,528,128]{2,1,0:T(8,128)(2,1)}, bf16[8,528,128]{2,1,0:T(8,128)(2,1)S(1)}, u32[]{:S(2)}, u32[]{:S(2)}) collective-permute-start(bf16[8,528,128]{2,1,0:T(8,128)(2,1)} %get-tuple-element.52), channel_id=1, source_target_pairs={{0,8},{1,9},{2,10},{3,11},{4,12},{5,13},{6,14},{7,15},{8,16},{9,17... | collective-permute-start | bytes 3244040 | tf_op jit(solution)/shard_map/ppermute | solution.py:552
  137.0 52.4 %collective-permute-start.1 = (bf16[8,528,128]{2,1,0:T(8,128)(2,1)}, bf16[8,528,128]{2,1,0:T(8,128)(2,1)S(1)}, u32[]{:S(2)}, u32[]{:S(2)}) collective-permute-start(bf16[8,528,128]{2,1,0:T(8,128)(2,1)} %get-tuple-element.53), channel_id=1, source_target_pairs={{0,16},{1,17},{2,18},{3,19},{4,20},{5,21},{6,22},{7,23},{8,24},{9,... | collective-permute-start | bytes 3244040 | tf_op jit(solution)/shard_map/ppermute | solution.py:552
  139.3 18.2 %collective-permute-start.3 = (bf16[3,528,128]{2,1,0:T(8,128)(2,1)S(1)}, bf16[3,528,128]{2,1,0:T(8,128)(2,1)S(1)}, u32[]{:S(2)}, u32[]{:S(2)}) collective-permute-start(bf16[3,528,128]{2,1,0:T(8,128)(2,1)S(1)} %copy-done.7), channel_id=1, source_target_pairs={{0,1},{1,2},{2,3},{3,4},{4,5},{5,6},{6,7},{7,0},{8,9},{9,10},{10,1... | collective-permute-start | bytes 1216520 | tf_op jit(solution)/shard_map/ppermute | solution.py:547
  143.1 38.8 %collective-permute-start.4 = (bf16[3,528,128]{2,1,0:T(8,128)(2,1)S(1)}, bf16[3,528,128]{2,1,0:T(8,128)(2,1)S(1)}, u32[]{:S(2)}, u32[]{:S(2)}) collective-permute-start(bf16[3,528,128]{2,1,0:T(8,128)(2,1)S(1)} %copy-done.6), channel_id=1, source_target_pairs={{0,2},{1,3},{2,4},{3,5},{4,6},{5,7},{6,0},{7,1},{8,10},{9,11},{10,... | collective-permute-start | bytes 1216520 | tf_op jit(solution)/shard_map/ppermute | solution.py:547
  157.5 34.3 %copy-start.11 = (bf16[3,528,128]{2,1,0:T(8,128)(2,1)}, bf16[3,528,128]{2,1,0:T(8,128)(2,1)S(1)}, u32[]{:S(2)}) copy-start(bf16[3,528,128]{2,1,0:T(8,128)(2,1)S(1)} %collective-permute-done.3.rest_1_) | copy-start | bytes 1216516
  157.5 113.4 %collective-permute-start.5 = (bf16[3,528,128]{2,1,0:T(8,128)(2,1)S(1)}, bf16[3,528,128]{2,1,0:T(8,128)(2,1)S(1)}, u32[]{:S(2)}, u32[]{:S(2)}) collective-permute-start(bf16[3,528,128]{2,1,0:T(8,128)(2,1)S(1)} %copy-done.5), channel_id=1, source_target_pairs={{0,3},{1,4},{2,5},{3,6},{4,7},{5,0},{6,1},{7,2},{8,11},{9,12},{10,... | collective-permute-start | bytes 1216520 | tf_op jit(solution)/shard_map/ppermute | solution.py:547
  181.9 9.9 %copy-start.12 = (bf16[3,528,128]{2,1,0:T(8,128)(2,1)}, bf16[3,528,128]{2,1,0:T(8,128)(2,1)S(1)}, u32[]{:S(2)}) copy-start(bf16[3,528,128]{2,1,0:T(8,128)(2,1)S(1)} %collective-permute-done.4.rest_2_) | copy-start | bytes 1216516
  181.9 89.1 %collective-permute-start.6 = (bf16[3,528,128]{2,1,0:T(8,128)(2,1)S(1)}, bf16[3,528,128]{2,1,0:T(8,128)(2,1)}, u32[]{:S(2)}, u32[]{:S(2)}) collective-permute-start(bf16[3,528,128]{2,1,0:T(8,128)(2,1)S(1)} %copy-done.4), channel_id=1, source_target_pairs={{0,4},{1,5},{2,6},{3,7},{4,0},{5,1},{6,2},{7,3},{8,12},{9,13},{10,... | collective-permute-start | bytes 1216520 | tf_op jit(solution)/shard_map/ppermute | solution.py:547
  181.9 79.9 %copy-start.8 = (bf16[8,528,128]{2,1,0:T(8,128)(2,1)}, bf16[8,528,128]{2,1,0:T(8,128)(2,1)S(1)}, u32[]{:S(2)}) copy-start(bf16[8,528,128]{2,1,0:T(8,128)(2,1)S(1)} %collective-permute-done.2.b3) | copy-start | bytes 3244036
  181.9 89.0 %collective-permute-start.7 = (bf16[3,528,128]{2,1,0:T(8,128)(2,1)S(1)}, bf16[3,528,128]{2,1,0:T(8,128)(2,1)}, u32[]{:S(2)}, u32[]{:S(2)}) collective-permute-start(bf16[3,528,128]{2,1,0:T(8,128)(2,1)S(1)} %copy-done.3), channel_id=1, source_target_pairs={{0,5},{1,6},{2,7},{3,0},{4,1},{5,2},{6,3},{7,4},{8,13},{9,14},{10,... | collective-permute-start | bytes 1216520 | tf_op jit(solution)/shard_map/ppermute | solution.py:547
  185.3 6.5 %copy-start.9 = (bf16[8,528,128]{2,1,0:T(8,128)(2,1)}, bf16[8,528,128]{2,1,0:T(8,128)(2,1)S(1)}, u32[]{:S(2)}) copy-start(bf16[8,528,128]{2,1,0:T(8,128)(2,1)S(1)} %collective-permute-done.b1) | copy-start | bytes 3244036
  185.3 85.7 %collective-permute-start.8 = (bf16[3,528,128]{2,1,0:T(8,128)(2,1)S(1)}, bf16[3,528,128]{2,1,0:T(8,128)(2,1)}, u32[]{:S(2)}, u32[]{:S(2)}) collective-permute-start(bf16[3,528,128]{2,1,0:T(8,128)(2,1)S(1)} %copy-done.2), channel_id=1, source_target_pairs={{0,6},{1,7},{2,0},{3,1},{4,2},{5,3},{6,4},{7,5},{8,14},{9,15},{10,... | collective-permute-start | bytes 1216520 | tf_op jit(solution)/shard_map/ppermute | solution.py:547
  189.3 2.5 copy-start.10
  189.3 81.6 %collective-permute-start.9 = (bf16[3,528,128]{2,1,0:T(8,128)(2,1)S(1)}, bf16[3,528,128]{2,1,0:T(8,128)(2,1)}, u32[]{:S(2)}, u32[]{:S(2)}) collective-permute-start(bf16[3,528,128]{2,1,0:T(8,128)(2,1)S(1)} %copy-done.1), channel_id=1, source_target_pairs={{0,7},{1,0},{2,1},{3,2},{4,3},{5,4},{6,5},{7,6},{8,15},{9,8},{10,9... | collective-permute-start | bytes 1216520 | tf_op jit(solution)/shard_map/ppermute | solution.py:547
  270.9 0.8 copy-start.13
  271.7 19.0 %copy-start = (f32[1024,128]{1,0:T(8,128)S(1)}, f32[1024,128]{1,0:T(8,128)}, u32[]{:S(2)}) copy-start(f32[1024,128]{1,0:T(8,128)} %total.1) | copy-start | bytes 1572868

commit v3 on v2

--- a/solution.py
+++ b/solution.py
@@ -263,7 +263,8 @@
         copy.start()
     acc[...] = jnp.zeros(acc.shape, F32)
     for k in range(KINDS):
-        turned_weight[k * 128 : (k + 1) * 128, :] = jnp.transpose(weight_ref[k])
+        half, kk = k // 4, k % 4
+        turned_weight[kk * 128 : (kk + 1) * 128, half * 128 : (half + 1) * 128] = jnp.transpose(weight_ref[k])
 
     def widen(i, c):
         at = pl.ds(pl.multiple_of(i * 512, 512), 512)
@@ -277,7 +278,7 @@
     for m, out_ref in enumerate(outs):
         q = (y + distances[m]) & (NY - 1)
 
-        def block(r, c, m=m, q=q, out_ref=out_ref):
+        def block(r, c, m_at=m, q=q, out_ref=out_ref):
             zz = (z + r) & (NZ - 1)
             at = q * NZ + zz
             base = at * 1024
@@ -290,20 +291,29 @@
                 return c
 
             lax.fori_loop(lo // 16, (hi + 15) // 16, group, 0)
-            codes = jnp.transpose((codes_ref[at] >> 14).astype(F32))
+            codes = (codes_ref[at] >> 14).astype(F32)
+            columns = jnp.transpose(codes)
 
             def piece(first, last):
+                n = last - first
                 cols = range(first // 128, (last + 127) // 128)
-                kinds = [jnp.broadcast_to(codes[: min(128, last - m * 128), m : m + 1], (min(128, last - m * 128), 128)) for m in cols]
+                tall = [min(128, last - m * 128) for m in cols]
+                kinds = [jnp.broadcast_to(columns[:t, m : m + 1], (t, 128)) for m, t in zip(cols, tall)]
                 kinds = jnp.concatenate(kinds, axis=0)
+                upper = kinds >= 4.0
+                quarter = jnp.where(upper, kinds - 4.0, kinds)
                 rows = rowbuf[first:last, :]
                 none = jnp.zeros(rows.shape, F32)
-                placed = [jnp.where(kinds == k, rows, none).astype(BF16) for k in range(KINDS)]
+                placed = [jnp.where(quarter == kk, rows, none).astype(BF16) for kk in range(4)]
                 placed = jnp.concatenate(placed, axis=1)
-                grads = jnp.dot(placed, turned_weight[...], preferred_element_type=F32)
-                out_ref[zz, first:last, :] = grads.astype(BF16)
-                turned = jnp.transpose(feats[r, m, first:last, :])
-                acc[...] += jnp.dot(turned, placed, preferred_element_type=F32)
+                both = jnp.dot(placed, turned_weight[...], preferred_element_type=F32)
+                out_ref[zz, first:last, :] = jnp.where(upper, both[:, 128:], both[:, :128]).astype(BF16)
+                turned = jnp.transpose(feats[r, m_at, first:last, :]).astype(F32)
+                across = jnp.concatenate([codes[m : m + 1, :] for m in cols], axis=1)[:, :n]
+                upper = jnp.broadcast_to(across, (128, n)) >= 4.0
+                none = jnp.zeros((128, n), F32)
+                split = [jnp.where(upper, none, turned).astype(BF16), jnp.where(upper, turned, none).astype(BF16)]
+                acc[...] += jnp.dot(jnp.concatenate(split, axis=0), placed, preferred_element_type=F32)
 
             piece(0, 256)
 
@@ -315,8 +325,8 @@
 
         lax.fori_loop(0, NZ, block, 0)
     for k in range(KINDS):
-        part = slice(k * 128, (k + 1) * 128)
-        term_ref[part, :] = acc[:, part]
+        half, kk = k // 4, k % 4
+        term_ref[k * 128 : (k + 1) * 128, :] = acc[half * 128 : (half + 1) * 128, kk * 128 : (kk + 1) * 128]
 
 
 def proxy(distances, want, table, weight, blocks, parts):
@@ -331,8 +341,8 @@
             pltpu.VMEM((NZ * PAR, 128), F32),
             pltpu.VMEM((CAP, 128), F32),
             pltpu.VMEM((NZ, n, CAP, 128), BF16),
-            pltpu.VMEM((128, KINDS * 128), F32),
-            pltpu.VMEM((KINDS * 128, 128), BF16),
+            pltpu.VMEM((256, 512), F32),
+            pltpu.VMEM((512, 256), BF16),
             pltpu.SemaphoreType.DMA((NZ, n)),
         ],
         compiler_params=pltpu.CompilerParams(vmem_limit_bytes=VLIM),
@@ -514,7 +524,16 @@
                 return c
 
             begin, end = (lo + 15) // 16, hi // 16
-            lax.fori_loop(begin, end, plain, 0)
+            fours = jnp.maximum(end - begin, 0) // 4
+
+            def four(g, c):
+                t = begin + g * 4
+                src = pl.ds(pl.multiple_of(t * 16, 16), 64)
+                out_ref[pl.ds(pl.multiple_of(first + t * 16, 16), 64), :] = back_ref[b, src, :]
+                return c
+
+            lax.fori_loop(0, fours, four, 0)
+            lax.fori_loop(begin + fours * 4, end, plain, 0)
             lax.fori_loop(lo // 16, jnp.minimum(lo // 16 + 1, (hi + 15) // 16), tile, 0)
             lax.fori_loop(jnp.maximum(end, lo // 16 + 1), (hi + 15) // 16, tile, 0)
             return c

time: 295 us -> 292 us (0.990)
  Pallas kernels: 230 us -> 226 us
where the time goes in v3:
time: 292 us; the launch traced here: 288 us
  Pallas kernels  226 us (77%)
  waiting for transfers between devices  37.7 us (13%)
  starting transfers between devices  21.4 us (7%)
    pallas_call x1, Pallas kernels, exchange(): pl.pallas_call(exchange_kernel, out_shape=(jax.ShapeDtypeStruct((NZ, PAR,...  77.3 us
    pallas_call x1, Pallas kernels, total(): pl.pallas_call(lambda *refs: total_kernel(scale, *refs), out_shape=jax.Sh...  69.6 us
    pallas_call x2, Pallas kernels, proxy(): pl.pallas_call(lambda *refs: proxy_kernel(distances, *refs), out_shape=(j...  47.5 us
    ppermute x7, waiting for transfers between devices, along_z(): lax.ppermute(v, 'space', [(d, d // NZ * NZ + (d + s) % NZ) for d in range...  37.7 us
    pallas_call x1, Pallas kernels, owner(): pl.pallas_call(owner_kernel, out_shape=jax.ShapeDtypeStruct((PAR, 128), B...  19 us
    ppermute x7, starting transfers between devices, along_z(): lax.ppermute(v, 'space', [(d, d // NZ * NZ + (d + s) % NZ) for d in range...  14.7 us
    ppermute x3, starting transfers between devices, along_y(): return lax.ppermute(v, 'space', [(d, (d + i * NZ) % NS) for d in range(NS)])  6.77 us
    pallas_call x1, Pallas kernels, unpack(): pl.pallas_call(unpack_kernel, out_shape=jax.ShapeDtypeStruct((rows, 128),...  6.7 us
  transfers between devices with their start and end apart: 10, of which 2 were waited for; matrix products, arithmetic and copies ran while one was open for 0% of the time, Pallas kernels for 35%

profile of v3, /device:TPU:2, one launch (start us, length us, event | category | flops | bytes accessed | tf_op | source)
XLA Modules:
  0.0 287.8 jit_solution(5043929553134881401)
XLA Ops:
  0.6 6.2 %pack.1 = (bf16[32,528,128]{2,1,0:T(8,128)(2,1)}, s32[32,8,128]{2,1,0:T(8,128)}, s32[32,8,128]{2,1,0:T(8,128)}, s32[32]{0:T(128)}, s32[32]{0:T(128)}, /*index=5*/s32[32]{0:T(128)}) custom-call(s32[64,128]{1,0:T(8,128)} %bitcast.22, s32[64,128]{1,0:T(8,128)} %bitcast.23, bf16[8192,128]{1,0:T(8,128)(2,1)} %bitcast.17), custom_call_target="tpu_custom_call" | custom-call | bytes 28800000 | tf_op jit(solution)/shard_map/pack/pallas_call | solution.py:83
  6.9 77.3 %exchange.1 = (bf16[8,2048,128]{2,1,0:T(8,128)(2,1)}, s32[32,8,128]{2,1,0:T(8,128)}, s32[32,8,128]{2,1,0:T(8,128)}, bf16[8,528,128]{2,1,0:T(8,128)(2,1)}, bf16[3...) custom-call(bf16[2048,128]{1,0:T(8,128)(2,1)} %bitcast.19, ...), custom_call_target="tpu_custom_call" | custom-call | bytes 180000000 | tf_op jit(solution)/shard_map/exchange/pallas_call | solution.py:232
  84.1 23.8 %proxy.3 = (bf16[8,528,128]{2,1,0:T(8,128)(2,1)}, bf16[8,528,128]{2,1,0:T(8,128)(2,1)}, f32[1024,128]{1,0:T(8,128)}) custom-call(s32[32768]{0:T(1024)} %bitcast.14, s32[32,8,128]{2,1,0:T(8,128)} %get-tuple-element.36.refs_1_, bf16[16384,128]{1,0:T(8,128)(2,1)} %bitcast.11, bf16[8,128,128]{2,1,0:T(8,128)(2,1)} %refs_3_.3, ...), custom_call_target="tpu_custom_call" | custom-call | bytes 72000000 | tf_op jit(solution)/shard_map/proxy/pallas_call | solution.py:334
  108.1 2.2 collective-permute-start.2
  110.2 23.6 %proxy.2 = (bf16[8,528,128]{2,1,0:T(8,128)(2,1)}, bf16[8,528,128]{2,1,0:T(8,128)(2,1)}, f32[1024,128]{1,0:T(8,128)}) custom-call(s32[32768]{0:T(1024)} %bitcast.15, s32[32,8,128]{2,1,0:T(8,128)} %get-tuple-element.36.refs_1_, bf16[16384,128]{1,0:T(8,128)(2,1)} %bitcast.12, bf16[8,128,128]{2,1,0:T(8,128)(2,1)} %refs_3_.3, ...), custom_call_target="tpu_custom_call" | custom-call | bytes 72000000 | tf_op jit(solution)/shard_map/proxy/pallas_call | solution.py:334
  133.9 2.2 collective-permute-start
  136.1 2.3 collective-permute-start.1
  138.5 3.7 %collective-permute-start.3 = (bf16[3,528,128]{2,1,0:T(8,128)(2,1)S(1)}, bf16[3,528,128]{2,1,0:T(8,128)(2,1)S(1)}, u32[]{:S(2)}, u32[]{:S(2)}) collective-permute-start(bf16[3,528,128]{2,1,0:T(8,128)(2,1)S(1)} %copy-done.7), channel_id=1, source_target_pairs={{0,1},{1,2},{2,3},{3,4},{4,5},{5,6},{6,7},{7,0},{8,9},{9,10},{10,1... | collective-permute-start | bytes 1216520 | tf_op jit(solution)/shard_map/ppermute | solution.py:566
  142.1 0.0 collective-permute-start.4
  142.1 14.5 %collective-permute-done.3.rest_1_ = bf16[3,528,128]{2,1,0:T(8,128)(2,1)S(1)} collective-permute-done((bf16[3,528,128]{2,1,0:T(8,128)(2,1)S(1)}, bf16[3,528,128]{2,1,0:T(8,128)(2,1)S(1)}, u32[]{:S(2)}, u32[]{:S(2)}) %collective-permute-start.3) | collective-permute-done | bytes 405536 | tf_op jit(solution)/shard_map/ppermute | solution.py:566
  156.7 1.6 collective-permute-start.5
  158.3 23.1 %collective-permute-done.4.rest_2_ = bf16[3,528,128]{2,1,0:T(8,128)(2,1)S(1)} collective-permute-done((bf16[3,528,128]{2,1,0:T(8,128)(2,1)S(1)}, bf16[3,528,128]{2,1,0:T(8,128)(2,1)S(1)}, u32[]{:S(2)}, u32[]{:S(2)}) %collective-permute-start.4) | collective-permute-done | bytes 405536 | tf_op jit(solution)/shard_map/ppermute | solution.py:566
  181.4 0.0 collective-permute-start.6
  181.5 2.7 collective-permute-start.7
  184.2 3.7 %collective-permute-start.8 = (bf16[3,528,128]{2,1,0:T(8,128)(2,1)S(1)}, bf16[3,528,128]{2,1,0:T(8,128)(2,1)}, u32[]{:S(2)}, u32[]{:S(2)}) collective-permute-start(bf16[3,528,128]{2,1,0:T(8,128)(2,1)S(1)} %copy-done.2), channel_id=1, source_target_pairs={{0,6},{1,7},{2,0},{3,1},{4,2},{5,3},{6,4},{7,5},{8,14},{9,15},{10,... | collective-permute-start | bytes 1216520 | tf_op jit(solution)/shard_map/ppermute | solution.py:566
  188.0 0.0 collective-permute-done.1.b2
  188.0 2.9 %collective-permute-start.9 = (bf16[3,528,128]{2,1,0:T(8,128)(2,1)S(1)}, bf16[3,528,128]{2,1,0:T(8,128)(2,1)}, u32[]{:S(2)}, u32[]{:S(2)}) collective-permute-start(bf16[3,528,128]{2,1,0:T(8,128)(2,1)S(1)} %copy-done.1), channel_id=1, source_target_pairs={{0,7},{1,0},{2,1},{3,2},{4,3},{5,4},{6,5},{7,6},{8,15},{9,8},{10,9... | collective-permute-start | bytes 1216520 | tf_op jit(solution)/shard_map/ppermute | solution.py:566
  190.9 69.6 %total.1 = f32[1024,128]{1,0:T(8,128)} custom-call(f32[1024,128]{1,0:T(8,128)} %get-tuple-element.46.refs_0_, f32[1024,128]{1,0:T(8,128)} %get-tuple-element.47.refs_1_), custom_call_target="tpu_custom_call" | custom-call | bytes 118800000 | tf_op jit(solution)/shard_map/total/pallas_call | solution.py:480
  260.5 6.7 %unpack.1 = bf16[8192,128]{1,0:T(8,128)(2,1)} custom-call(s32[32]{0:T(128)} %get-tuple-element.48.first_ref, s32[32]{0:T(128)} %get-tuple-element.49.lo_ref, s32[32]{0:T(128)} %get-tuple-element.50.hi_ref, bf16[8,528,128]{2,1,0:T(8,128)(2,1)} %get-tuple-element.51.b0, bf16[8,528,128]{2,1,0:T(8,128)(2,1)} %copy-done.9, bf16[8,528,128]{2,1,0:T(8,128)(2,1)} %copy-done.10, ...), custom_call_target="tpu_custom_call" | custom-call | bytes 28800000 | tf_op jit(solution)/shard_map/unpack/pallas_call | solution.py:545
  267.2 0.0 collective-permute-done.5.rest_3_
  267.2 0.0 collective-permute-done.6.rest_4_
  267.3 0.7 copy-done.13
  268.0 19.0 %owner.1 = bf16[2048,128]{1,0:T(8,128)(2,1)} custom-call(s32[32768]{0:T(1024)} %bitcast.21, bf16[1024,128]{1,0:T(8,128)(2,1)} %bitcast.13, bf16[32,528,128]{2,1,0:T(8,128)(2,1)} %get-tuple-element.33.blk_ref.refs_4_, bf16[8,528,128]{2,1,0:T(8,128)(2,1)} %get-tuple-element.56.near_ref, bf16[3,528,128]{2,1,0:T(8,128)(2,1)} %get-tuple-element.38.refs_5_.rest_0_, ...), custom_call_target="tpu_custom_call" | custom-call | bytes 64800000 | tf_op jit(solution)/shard_map/owner/pallas_call | solution.py:409
  287.0 0.8 copy.9
  (32 shorter events, 0.1 us)
Async XLA Ops:
  108.0 30.5 %copy-start.7 = (bf16[3,528,128]{2,1,0:T(8,128)(2,1)S(1)}, bf16[3,528,128]{2,1,0:T(8,128)(2,1)}, u32[]{:S(2)}) copy-start(bf16[3,528,128]{2,1,0:T(8,128)(2,1)} %get-tuple-element.39.refs_6_) | copy-start | bytes 1216516
  108.0 34.1 %copy-start.6 = (bf16[3,528,128]{2,1,0:T(8,128)(2,1)S(1)}, bf16[3,528,128]{2,1,0:T(8,128)(2,1)}, u32[]{:S(2)}) copy-start(bf16[3,528,128]{2,1,0:T(8,128)(2,1)} %get-tuple-element.40.refs_7_) | copy-start | bytes 1216516
  108.0 48.7 %copy-start.5 = (bf16[3,528,128]{2,1,0:T(8,128)(2,1)S(1)}, bf16[3,528,128]{2,1,0:T(8,128)(2,1)}, u32[]{:S(2)}) copy-start(bf16[3,528,128]{2,1,0:T(8,128)(2,1)} %get-tuple-element.41.refs_8_) | copy-start | bytes 1216516
  108.0 73.4 %copy-start.4 = (bf16[3,528,128]{2,1,0:T(8,128)(2,1)S(1)}, bf16[3,528,128]{2,1,0:T(8,128)(2,1)}, u32[]{:S(2)}) copy-start(bf16[3,528,128]{2,1,0:T(8,128)(2,1)} %get-tuple-element.42.refs_9_) | copy-start | bytes 1216516
  108.0 73.4 %copy-start.3 = (bf16[3,528,128]{2,1,0:T(8,128)(2,1)S(1)}, bf16[3,528,128]{2,1,0:T(8,128)(2,1)}, u32[]{:S(2)}) copy-start(bf16[3,528,128]{2,1,0:T(8,128)(2,1)} %get-tuple-element.43.refs_10_) | copy-start | bytes 1216516
  108.0 76.2 %copy-start.2 = (bf16[3,528,128]{2,1,0:T(8,128)(2,1)S(1)}, bf16[3,528,128]{2,1,0:T(8,128)(2,1)}, u32[]{:S(2)}) copy-start(bf16[3,528,128]{2,1,0:T(8,128)(2,1)} %get-tuple-element.44.refs_11_) | copy-start | bytes 1216516
  108.0 79.9 %copy-start.1 = (bf16[3,528,128]{2,1,0:T(8,128)(2,1)S(1)}, bf16[3,528,128]{2,1,0:T(8,128)(2,1)}, u32[]{:S(2)}) copy-start(bf16[3,528,128]{2,1,0:T(8,128)(2,1)} %get-tuple-element.45.refs_12_) | copy-start | bytes 1216516
  108.1 73.4 %collective-permute-start.2 = (bf16[8,528,128]{2,1,0:T(8,128)(2,1)}, bf16[8,528,128]{2,1,0:T(8,128)(2,1)S(1)}, u32[]{:S(2)}, u32[]{:S(2)}) collective-permute-start(bf16[8,528,128]{2,1,0:T(8,128)(2,1)} %get-tuple-element.54), channel_id=1, source_target_pairs={{0,24},{1,25},{2,26},{3,27},{4,28},{5,29},{6,30},{7,31},{8,0},{9,1... | collective-permute-start | bytes 3244040 | tf_op jit(solution)/shard_map/ppermute | solution.py:571
  133.9 50.3 %collective-permute-start = (bf16[8,528,128]{2,1,0:T(8,128)(2,1)}, bf16[8,528,128]{2,1,0:T(8,128)(2,1)S(1)}, u32[]{:S(2)}, u32[]{:S(2)}) collective-permute-start(bf16[8,528,128]{2,1,0:T(8,128)(2,1)} %get-tuple-element.52), channel_id=1, source_target_pairs={{0,8},{1,9},{2,10},{3,11},{4,12},{5,13},{6,14},{7,15},{8,16},{9,17... | collective-permute-start | bytes 3244040 | tf_op jit(solution)/shard_map/ppermute | solution.py:571
  136.1 51.9 %collective-permute-start.1 = (bf16[8,528,128]{2,1,0:T(8,128)(2,1)}, bf16[8,528,128]{2,1,0:T(8,128)(2,1)S(1)}, u32[]{:S(2)}, u32[]{:S(2)}) collective-permute-start(bf16[8,528,128]{2,1,0:T(8,128)(2,1)} %get-tuple-element.53), channel_id=1, source_target_pairs={{0,16},{1,17},{2,18},{3,19},{4,20},{5,21},{6,22},{7,23},{8,24},{9,... | collective-permute-start | bytes 3244040 | tf_op jit(solution)/shard_map/ppermute | solution.py:571
  138.5 18.2 %collective-permute-start.3 = (bf16[3,528,128]{2,1,0:T(8,128)(2,1)S(1)}, bf16[3,528,128]{2,1,0:T(8,128)(2,1)S(1)}, u32[]{:S(2)}, u32[]{:S(2)}) collective-permute-start(bf16[3,528,128]{2,1,0:T(8,128)(2,1)S(1)} %copy-done.7), channel_id=1, source_target_pairs={{0,1},{1,2},{2,3},{3,4},{4,5},{5,6},{6,7},{7,0},{8,9},{9,10},{10,1... | collective-permute-start | bytes 1216520 | tf_op jit(solution)/shard_map/ppermute | solution.py:566
  142.1 39.3 %collective-permute-start.4 = (bf16[3,528,128]{2,1,0:T(8,128)(2,1)S(1)}, bf16[3,528,128]{2,1,0:T(8,128)(2,1)S(1)}, u32[]{:S(2)}, u32[]{:S(2)}) collective-permute-start(bf16[3,528,128]{2,1,0:T(8,128)(2,1)S(1)} %copy-done.6), channel_id=1, source_target_pairs={{0,2},{1,3},{2,4},{3,5},{4,6},{5,7},{6,0},{7,1},{8,10},{9,11},{10,... | collective-permute-start | bytes 1216520 | tf_op jit(solution)/shard_map/ppermute | solution.py:566
  156.7 34.2 %copy-start.11 = (bf16[3,528,128]{2,1,0:T(8,128)(2,1)}, bf16[3,528,128]{2,1,0:T(8,128)(2,1)S(1)}, u32[]{:S(2)}) copy-start(bf16[3,528,128]{2,1,0:T(8,128)(2,1)S(1)} %collective-permute-done.3.rest_1_) | copy-start | bytes 1216516
  156.7 110.6 %collective-permute-start.5 = (bf16[3,528,128]{2,1,0:T(8,128)(2,1)S(1)}, bf16[3,528,128]{2,1,0:T(8,128)(2,1)S(1)}, u32[]{:S(2)}, u32[]{:S(2)}) collective-permute-start(bf16[3,528,128]{2,1,0:T(8,128)(2,1)S(1)} %copy-done.5), channel_id=1, source_target_pairs={{0,3},{1,4},{2,5},{3,6},{4,7},{5,0},{6,1},{7,2},{8,11},{9,12},{10,... | collective-permute-start | bytes 1216520 | tf_op jit(solution)/shard_map/ppermute | solution.py:566
  181.4 9.4 %copy-start.12 = (bf16[3,528,128]{2,1,0:T(8,128)(2,1)}, bf16[3,528,128]{2,1,0:T(8,128)(2,1)S(1)}, u32[]{:S(2)}) copy-start(bf16[3,528,128]{2,1,0:T(8,128)(2,1)S(1)} %collective-permute-done.4.rest_2_) | copy-start | bytes 1216516
  181.4 85.8 %collective-permute-start.6 = (bf16[3,528,128]{2,1,0:T(8,128)(2,1)S(1)}, bf16[3,528,128]{2,1,0:T(8,128)(2,1)}, u32[]{:S(2)}, u32[]{:S(2)}) collective-permute-start(bf16[3,528,128]{2,1,0:T(8,128)(2,1)S(1)} %copy-done.4), channel_id=1, source_target_pairs={{0,4},{1,5},{2,6},{3,7},{4,0},{5,1},{6,2},{7,3},{8,12},{9,13},{10,... | collective-permute-start | bytes 1216520 | tf_op jit(solution)/shard_map/ppermute | solution.py:566
  181.5 79.1 %copy-start.8 = (bf16[8,528,128]{2,1,0:T(8,128)(2,1)}, bf16[8,528,128]{2,1,0:T(8,128)(2,1)S(1)}, u32[]{:S(2)}) copy-start(bf16[8,528,128]{2,1,0:T(8,128)(2,1)S(1)} %collective-permute-done.2.b3) | copy-start | bytes 3244036
  181.5 85.8 %collective-permute-start.7 = (bf16[3,528,128]{2,1,0:T(8,128)(2,1)S(1)}, bf16[3,528,128]{2,1,0:T(8,128)(2,1)}, u32[]{:S(2)}, u32[]{:S(2)}) collective-permute-start(bf16[3,528,128]{2,1,0:T(8,128)(2,1)S(1)} %copy-done.3), channel_id=1, source_target_pairs={{0,5},{1,6},{2,7},{3,0},{4,1},{5,2},{6,3},{7,4},{8,13},{9,14},{10,... | collective-permute-start | bytes 1216520 | tf_op jit(solution)/shard_map/ppermute | solution.py:566
  184.2 6.6 %copy-start.9 = (bf16[8,528,128]{2,1,0:T(8,128)(2,1)}, bf16[8,528,128]{2,1,0:T(8,128)(2,1)S(1)}, u32[]{:S(2)}) copy-start(bf16[8,528,128]{2,1,0:T(8,128)(2,1)S(1)} %collective-permute-done.b1) | copy-start | bytes 3244036
  184.2 83.0 %collective-permute-start.8 = (bf16[3,528,128]{2,1,0:T(8,128)(2,1)S(1)}, bf16[3,528,128]{2,1,0:T(8,128)(2,1)}, u32[]{:S(2)}, u32[]{:S(2)}) collective-permute-start(bf16[3,528,128]{2,1,0:T(8,128)(2,1)S(1)} %copy-done.2), channel_id=1, source_target_pairs={{0,6},{1,7},{2,0},{3,1},{4,2},{5,3},{6,4},{7,5},{8,14},{9,15},{10,... | collective-permute-start | bytes 1216520 | tf_op jit(solution)/shard_map/ppermute | solution.py:566
  188.0 2.9 %copy-start.10 = (bf16[8,528,128]{2,1,0:T(8,128)(2,1)}, bf16[8,528,128]{2,1,0:T(8,128)(2,1)S(1)}, u32[]{:S(2)}) copy-start(bf16[8,528,128]{2,1,0:T(8,128)(2,1)S(1)} %collective-permute-done.1.b2) | copy-start | bytes 3244036
  188.0 79.3 %collective-permute-start.9 = (bf16[3,528,128]{2,1,0:T(8,128)(2,1)S(1)}, bf16[3,528,128]{2,1,0:T(8,128)(2,1)}, u32[]{:S(2)}, u32[]{:S(2)}) collective-permute-start(bf16[3,528,128]{2,1,0:T(8,128)(2,1)S(1)} %copy-done.1), channel_id=1, source_target_pairs={{0,7},{1,0},{2,1},{3,2},{4,3},{5,4},{6,5},{7,6},{8,15},{9,8},{10,9... | collective-permute-start | bytes 1216520 | tf_op jit(solution)/shard_map/ppermute | solution.py:566
  267.2 0.8 copy-start.13
  268.0 19.0 %copy-start = (f32[1024,128]{1,0:T(8,128)S(1)}, f32[1024,128]{1,0:T(8,128)}, u32[]{:S(2)}) copy-start(f32[1024,128]{1,0:T(8,128)} %total.1) | copy-start | bytes 1572868

commit v4 on v3

--- a/solution.py
+++ b/solution.py
@@ -22,6 +22,7 @@
 VM = pl.BlockSpec(memory_space=pltpu.VMEM)
 SM = pl.BlockSpec(memory_space=pltpu.SMEM)
 VLIM = 60 * 1024 * 1024
+LATE = (3, 4, 5)
 
 
 def cost(us):
@@ -178,7 +179,7 @@
             device_id_type=MESH,
         )
 
-    straights = [straight(r) for r in (1, 7, 2, 6, 3, 5, 4)]
+    straights = [straight(r) for r in range(1, NZ) if r not in LATE]
 
     def slots_to(i):
         t = lax.rem(me + i, NS)
@@ -352,14 +353,20 @@
     return dict(zip(distances, rows)), term
 
 
-def owner_kernel(slot_ref, weight_ref, blk_ref, near_ref, *rest):
+def owner_kernel(slot_ref, weight_ref, blk_ref, near_ref, late_ref, *rest):
     parts = rest[:NZ]
     out_ref, grid_ref, rowbuf, feats, sems = rest[NZ:]
     y, z = place()
+
+    def straight(s):
+        if s == 0:
+            return blk_ref.at[y * NZ + z]
+        return late_ref.at[LATE.index(s)] if s in LATE else near_ref.at[s]
+
     copies = [
         (
             pltpu.make_async_copy(part, feats.at[s, pl.ds(1, NY - 1)], sems.at[s, 0]),
-            pltpu.make_async_copy(near_ref.at[s] if s else blk_ref.at[y * NZ + z], feats.at[s, 0], sems.at[s, 1]),
+            pltpu.make_async_copy(straight(s), feats.at[s, 0], sems.at[s, 1]),
         )
         for s, part in enumerate(parts)
     ]
@@ -405,11 +412,11 @@
     lax.fori_loop(0, PAR // 512, chunk, 0)
 
 
-def owner(slots, weight, blocks, near, parts):
+def owner(slots, weight, blocks, near, late, parts):
     return pl.pallas_call(
         owner_kernel,
         out_shape=jax.ShapeDtypeStruct((PAR, 128), BF16),
-        in_specs=[SM, VM] + [ANY] * (NZ + 2),
+        in_specs=[SM, VM] + [ANY] * (NZ + 3),
         out_specs=VM,
         scratch_shapes=[
             pltpu.VMEM((SLOTS + 8, 128), F32),
@@ -420,10 +427,12 @@
         compiler_params=pltpu.CompilerParams(vmem_limit_bytes=VLIM),
         cost_estimate=cost(18),
         name="owner",
-    )(slots.reshape(-1), weight, blocks, near, *parts)
-
-
-def total_kernel(scale, far_ref, near_ref, out_ref, term_ref, b1, s1, b2, s2, b3, s3, b4, s4, send, recv):
+    )(slots.reshape(-1), weight, blocks, near, late, *parts)
+
+
+def total_kernel(
+    scale, far_ref, near_ref, blk_ref, out_ref, late_ref, term_ref, b1, s1, b2, s2, b3, s3, b4, s4, send, recv, ls, lr
+):
     dp, me = lax.axis_index("dp"), lax.axis_index("space")
     y, z = me // NZ, lax.rem(me, NZ)
     at_dp = lambda i: (lax.rem(dp + i, ND), me)
@@ -467,21 +476,38 @@
     end(c)
     s3[...] = ((b3[0] + b3[1]) + (b3[2] + b3[3])) * scale
     c = swap(3, NZ, at_z, lambda i: s3, b4.at[rows(z, 16)])
+    late = [
+        pltpu.make_async_remote_copy(
+            blk_ref.at[y * NZ + lax.rem(z + r, NZ)],
+            late_ref.at[m],
+            ls.at[m],
+            lr.at[m],
+            device_id=at_z(r),
+            device_id_type=MESH,
+        )
+        for m, r in enumerate(LATE)
+    ]
+    for copy in late:
+        copy.start()
     b4[rows(z, 16), :] = s3[...]
     end(c)
     c = swap(4, ND, at_dp, lambda i: b4, s4.at[rows(dp, 128)])
     s4[rows(dp, 128), :] = b4[...]
     end(c)
     out_ref[...] = s4[...]
-
-
-def total(far, near, scale):
+    end(late)
+
+
+def total(far, near, blocks, scale):
     n = KINDS * 128
     return pl.pallas_call(
         lambda *refs: total_kernel(scale, *refs),
-        out_shape=jax.ShapeDtypeStruct((n, 128), F32),
-        in_specs=[VM, VM],
-        out_specs=VM,
+        out_shape=(
+            jax.ShapeDtypeStruct((n, 128), F32),
+            jax.ShapeDtypeStruct((len(LATE), CAP, 128), BF16),
+        ),
+        in_specs=[VM, VM, ANY],
+        out_specs=(VM, ANY),
         scratch_shapes=[
             pltpu.VMEM((n, 128), F32),
             pltpu.VMEM((ND, 128, 128), F32),
@@ -494,11 +520,13 @@
             pltpu.VMEM((n, 128), F32),
             pltpu.SemaphoreType.DMA((5, 8)),
             pltpu.SemaphoreType.DMA((5, 8)),
+            pltpu.SemaphoreType.DMA((len(LATE),)),
+            pltpu.SemaphoreType.DMA((len(LATE),)),
         ],
         compiler_params=pltpu.CompilerParams(collective_id=2, has_side_effects=True),
         cost_estimate=cost(33),
         name="total",
-    )(far, near)
+    )(far, near, blocks)
 
 
 def unpack_kernel(first_ref, lo_ref, hi_ref, b0, b1, b2, b3, out_ref):
@@ -577,11 +605,11 @@
     reply = {**far, **near}
     back = [along_y(reply[i], i) for i in range(NY)]
     grad_rows = fine_rows * NS * lax.axis_size("dp")
-    weight_grad = total(far_term, near_term, float(1.0 / grad_rows**0.5))
+    weight_grad, late_blocks = total(far_term, near_term, blocks, float(1.0 / grad_rows**0.5))
     first, weight_grad = lax.optimization_barrier((first, weight_grad))
     feature_grad = unpack(first, lo, hi, back, fine_rows)
     got, feature_grad = lax.optimization_barrier((got, feature_grad))
-    result = owner(got, weight.reshape(KINDS * 128, 128), blocks, near_blocks, arrived)
+    result = owner(got, weight.reshape(KINDS * 128, 128), blocks, near_blocks, late_blocks, arrived)
     return result[None], feature_grad[None], weight_grad.reshape(KINDS, 128, 128)
 
 

time: 292 us -> 279 us (0.955)
  Pallas kernels: 226 us -> 215 us
  starting transfers between devices: 21.4 us -> 17.1 us
    pallas_call x1, Pallas kernels: 77.3 us -> 64.4 us  [exchange(): pl.pallas_call(exchange_kernel, out_shape=(jax.ShapeDtypeStruct((NZ, PAR,...]
    ppermute x7, starting transfers between devices: 14.7 us -> 10.3 us  [along_z(): lax.ppermute(v, 'space', [(d, d // NZ * NZ + (d + s) % NZ) for d in range...]
    ppermute x3, waiting for transfers between devices: 0.01 us -> 2.96 us  [along_y(): return lax.ppermute(v, 'space', [(d, (d + i * NZ) % NS) for d in range(NS)])]
  transfers between devices with their start and end apart: 10 -> 10, of which waited for: 2 -> 3; matrix products, arithmetic and copies ran while one was open for 0% -> 0% of each run, Pallas kernels for 35% -> 37%
where the time goes in v4:
time: 279 us; the launch traced here: 274 us
  Pallas kernels  215 us (77%)
  waiting for transfers between devices  39.8 us (14%)
  starting transfers between devices  17.1 us (6%)
    pallas_call x1, Pallas kernels, total(): pl.pallas_call(lambda *refs: total_kernel(scale, *refs), out_shape=(jax.S...  71.1 us
    pallas_call x1, Pallas kernels, exchange(): pl.pallas_call(exchange_kernel, out_shape=(jax.ShapeDtypeStruct((NZ, PAR,...  64.4 us
    pallas_call x2, Pallas kernels, proxy(): pl.pallas_call(lambda *refs: proxy_kernel(distances, *refs), out_shape=(j...  47.5 us
    ppermute x7, waiting for transfers between devices, along_z(): lax.ppermute(v, 'space', [(d, d // NZ * NZ + (d + s) % NZ) for d in range...  36.9 us
    pallas_call x1, Pallas kernels, owner(): pl.pallas_call(owner_kernel, out_shape=jax.ShapeDtypeStruct((PAR, 128), B...  19 us
    ppermute x7, starting transfers between devices, along_z(): lax.ppermute(v, 'space', [(d, d // NZ * NZ + (d + s) % NZ) for d in range...  10.3 us
    ppermute x3, starting transfers between devices, along_y(): return lax.ppermute(v, 'space', [(d, (d + i * NZ) % NS) for d in range(NS)])  6.76 us
    pallas_call x1, Pallas kernels, unpack(): pl.pallas_call(unpack_kernel, out_shape=jax.ShapeDtypeStruct((rows, 128),...  6.7 us
  transfers between devices with their start and end apart: 10, of which 3 were waited for; matrix products, arithmetic and copies ran while one was open for 0% of the time, Pallas kernels for 37%

profile of v4, /device:TPU:2, one launch (start us, length us, event | category | flops | bytes accessed | tf_op | source)
XLA Modules:
  0.0 274.2 jit_solution(16008429425929888830)
XLA Ops:
  0.6 6.2 %pack.1 = (bf16[32,528,128]{2,1,0:T(8,128)(2,1)}, s32[32,8,128]{2,1,0:T(8,128)}, s32[32,8,128]{2,1,0:T(8,128)}, s32[32]{0:T(128)}, s32[32]{0:T(128)}, /*index=5*/s32[32]{0:T(128)}) custom-call(s32[64,128]{1,0:T(8,128)} %bitcast.22, s32[64,128]{1,0:T(8,128)} %bitcast.23, bf16[8192,128]{1,0:T(8,128)(2,1)} %bitcast.16), custom_call_target="tpu_custom_call" | custom-call | bytes 28800000 | tf_op jit(solution)/shard_map/pack/pallas_call | solution.py:84
  6.8 64.4 %exchange.1 = (bf16[8,2048,128]{2,1,0:T(8,128)(2,1)}, s32[32,8,128]{2,1,0:T(8,128)}, s32[32,8,128]{2,1,0:T(8,128)}, bf16[8,528,128]{2,1,0:T(8,128)(2,1)}, bf16[3...) custom-call(bf16[2048,128]{1,0:T(8,128)(2,1)} %bitcast.18, ...), custom_call_target="tpu_custom_call" | custom-call | bytes 180000000 | tf_op jit(solution)/shard_map/exchange/pallas_call | solution.py:233
  71.3 23.8 %proxy.3 = (bf16[8,528,128]{2,1,0:T(8,128)(2,1)}, bf16[8,528,128]{2,1,0:T(8,128)(2,1)}, f32[1024,128]{1,0:T(8,128)}) custom-call(s32[32768]{0:T(1024)} %bitcast.14, s32[32,8,128]{2,1,0:T(8,128)} %get-tuple-element.38.refs_1_, bf16[16384,128]{1,0:T(8,128)(2,1)} %bitcast.11, bf16[8,128,128]{2,1,0:T(8,128)(2,1)} %refs_3_.3, ...), custom_call_target="tpu_custom_call" | custom-call | bytes 72000000 | tf_op jit(solution)/shard_map/proxy/pallas_call | solution.py:335
  95.2 2.2 collective-permute-start.2
  97.4 23.6 %proxy.2 = (bf16[8,528,128]{2,1,0:T(8,128)(2,1)}, bf16[8,528,128]{2,1,0:T(8,128)(2,1)}, f32[1024,128]{1,0:T(8,128)}) custom-call(s32[32768]{0:T(1024)} %bitcast.15, s32[32,8,128]{2,1,0:T(8,128)} %get-tuple-element.38.refs_1_, bf16[16384,128]{1,0:T(8,128)(2,1)} %bitcast.12, bf16[8,128,128]{2,1,0:T(8,128)(2,1)} %refs_3_.3, ...), custom_call_target="tpu_custom_call" | custom-call | bytes 72000000 | tf_op jit(solution)/shard_map/proxy/pallas_call | solution.py:335
  121.0 2.2 collective-permute-start
  123.2 2.3 collective-permute-start.1
  125.6 1.7 collective-permute-start.3
  127.3 1.2 collective-permute-start.4
  128.5 17.5 %collective-permute-done.3.rest_1_ = bf16[3,528,128]{2,1,0:T(8,128)(2,1)S(1)} collective-permute-done((bf16[3,528,128]{2,1,0:T(8,128)(2,1)S(1)}, bf16[3,528,128]{2,1,0:T(8,128)(2,1)S(1)}, u32[]{:S(2)}, u32[]{:S(2)}) %collective-permute-start.3) | collective-permute-done | bytes 405536 | tf_op jit(solution)/shard_map/ppermute | solution.py:594
  146.0 19.4 %collective-permute-done.4.rest_2_ = bf16[3,528,128]{2,1,0:T(8,128)(2,1)S(1)} collective-permute-done((bf16[3,528,128]{2,1,0:T(8,128)(2,1)S(1)}, bf16[3,528,128]{2,1,0:T(8,128)(2,1)S(1)}, u32[]{:S(2)}, u32[]{:S(2)}) %collective-permute-start.4) | collective-permute-done | bytes 405536 | tf_op jit(solution)/shard_map/ppermute | solution.py:594
  165.4 0.0 collective-permute-done.2.b3
  165.4 3.4 %collective-permute-start.7 = (bf16[3,528,128]{2,1,0:T(8,128)(2,1)S(1)}, bf16[3,528,128]{2,1,0:T(8,128)(2,1)}, u32[]{:S(2)}, u32[]{:S(2)}) collective-permute-start(bf16[3,528,128]{2,1,0:T(8,128)(2,1)S(1)} %copy-done.2), channel_id=1, source_target_pairs={{0,5},{1,6},{2,7},{3,0},{4,1},{5,2},{6,3},{7,4},{8,13},{9,14},{10,... | collective-permute-start | bytes 1216520 | tf_op jit(solution)/shard_map/ppermute | solution.py:594
  168.8 3.0 %collective-permute-done.b1 = bf16[8,528,128]{2,1,0:T(8,128)(2,1)S(1)} collective-permute-done((bf16[8,528,128]{2,1,0:T(8,128)(2,1)}, bf16[8,528,128]{2,1,0:T(8,128)(2,1)S(1)}, u32[]{:S(2)}, u32[]{:S(2)}) %collective-permute-start) | collective-permute-done | bytes 1081376 | tf_op jit(solution)/shard_map/ppermute | solution.py:599
  171.8 0.0 collective-permute-done.1.b2
  171.8 4.0 %collective-permute-start.9 = (bf16[3,528,128]{2,1,0:T(8,128)(2,1)S(1)}, bf16[3,528,128]{2,1,0:T(8,128)(2,1)}, u32[]{:S(2)}, u32[]{:S(2)}) collective-permute-start(bf16[3,528,128]{2,1,0:T(8,128)(2,1)S(1)} %copy-done), channel_id=1, source_target_pairs={{0,7},{1,0},{2,1},{3,2},{4,3},{5,4},{6,5},{7,6},{8,15},{9,8},{10,9... | collective-permute-start | bytes 1216520 | tf_op jit(solution)/shard_map/ppermute | solution.py:594
  175.8 71.1 %total.1 = (f32[1024,128]{1,0:T(8,128)}, bf16[3,528,128]{2,1,0:T(8,128)(2,1)}) custom-call(f32[1024,128]{1,0:T(8,128)} %get-tuple-element.48.refs_0_, f32[1024,128]{1,0:T(8,128)} %get-tuple-element.49.refs_1_, bf16[32,528,128]{2,1,0:T(8,128)(2,1)} %get-tuple-element.35.blk_ref.refs_4_.refs_2_), custom_call_target="tpu_custom_call" | custom-call | bytes 118800000 | tf_op jit(solution)/shard_map/total/pallas_call | solution.py:503
  247.0 6.7 %unpack.1 = bf16[8192,128]{1,0:T(8,128)(2,1)} custom-call(s32[32]{0:T(128)} %get-tuple-element.51.first_ref, s32[32]{0:T(128)} %get-tuple-element.52.lo_ref, s32[32]{0:T(128)} %get-tuple-element.53.hi_ref, bf16[8,528,128]{2,1,0:T(8,128)(2,1)} %get-tuple-element.54.b0, bf16[8,528,128]{2,1,0:T(8,128)(2,1)} %copy-done.8, bf16[8,528,128]{2,1,0:T(8,128)(2,1)} %copy-done.9, ...), custom_call_target="tpu_custom_call" | custom-call | bytes 28800000 | tf_op jit(solution)/shard_map/unpack/pallas_call | solution.py:573
  253.7 0.0 collective-permute-done.5.rest_3_
  253.7 0.0 collective-permute-done.7.rest_5_
  253.7 0.0 collective-permute-done.8.rest_6_
  253.7 0.7 copy-done.13
  254.4 19.0 %owner.1 = bf16[2048,128]{1,0:T(8,128)(2,1)} custom-call(s32[32768]{0:T(1024)} %bitcast.21, bf16[1024,128]{1,0:T(8,128)(2,1)} %bitcast.13, bf16[32,528,128]{2,1,0:T(8,128)(2,1)} %get-tuple-element.35.blk_ref.refs_4_.refs_2_, bf16[8,528,128]{2,1,0:T(8,128)(2,1)} %get-tuple-element.59.near_ref, bf16[3,528,128]{2,1,0:T(8,128)(2,1)} %get-tuple-element.60.late_ref, ...), custom_call_target="tpu_custom_call" | custom-call | bytes 64800000 | tf_op jit(solution)/shard_map/owner/pallas_call | solution.py:416
  273.4 0.8 copy.9
  (32 shorter events, 0.1 us)
Async XLA Ops:
  95.1 30.5 %copy-start.6 = (bf16[3,528,128]{2,1,0:T(8,128)(2,1)S(1)}, bf16[3,528,128]{2,1,0:T(8,128)(2,1)}, u32[]{:S(2)}) copy-start(bf16[3,528,128]{2,1,0:T(8,128)(2,1)} %get-tuple-element.41.refs_6_) | copy-start | bytes 1216516
  95.1 32.2 %copy-start.5 = (bf16[3,528,128]{2,1,0:T(8,128)(2,1)S(1)}, bf16[3,528,128]{2,1,0:T(8,128)(2,1)}, u32[]{:S(2)}) copy-start(bf16[3,528,128]{2,1,0:T(8,128)(2,1)} %get-tuple-element.42.refs_7_) | copy-start | bytes 1216516
  95.1 50.8 %copy-start.4 = (bf16[3,528,128]{2,1,0:T(8,128)(2,1)S(1)}, bf16[3,528,128]{2,1,0:T(8,128)(2,1)}, u32[]{:S(2)}) copy-start(bf16[3,528,128]{2,1,0:T(8,128)(2,1)} %get-tuple-element.43.refs_8_) | copy-start | bytes 1216516
  95.1 70.2 %copy-start.3 = (bf16[3,528,128]{2,1,0:T(8,128)(2,1)S(1)}, bf16[3,528,128]{2,1,0:T(8,128)(2,1)}, u32[]{:S(2)}) copy-start(bf16[3,528,128]{2,1,0:T(8,128)(2,1)} %get-tuple-element.44.refs_9_) | copy-start | bytes 1216516
  95.1 70.3 %copy-start.2 = (bf16[3,528,128]{2,1,0:T(8,128)(2,1)S(1)}, bf16[3,528,128]{2,1,0:T(8,128)(2,1)}, u32[]{:S(2)}) copy-start(bf16[3,528,128]{2,1,0:T(8,128)(2,1)} %get-tuple-element.45.refs_10_) | copy-start | bytes 1216516
  95.2 76.6 %copy-start.1 = (bf16[3,528,128]{2,1,0:T(8,128)(2,1)S(1)}, bf16[3,528,128]{2,1,0:T(8,128)(2,1)}, u32[]{:S(2)}) copy-start(bf16[3,528,128]{2,1,0:T(8,128)(2,1)} %get-tuple-element.46.refs_11_) | copy-start | bytes 1216516
  95.2 76.7 %copy-start = (bf16[3,528,128]{2,1,0:T(8,128)(2,1)S(1)}, bf16[3,528,128]{2,1,0:T(8,128)(2,1)}, u32[]{:S(2)}) copy-start(bf16[3,528,128]{2,1,0:T(8,128)(2,1)} %get-tuple-element.47.refs_12_) | copy-start | bytes 1216516
  95.2 70.2 %collective-permute-start.2 = (bf16[8,528,128]{2,1,0:T(8,128)(2,1)}, bf16[8,528,128]{2,1,0:T(8,128)(2,1)S(1)}, u32[]{:S(2)}, u32[]{:S(2)}) collective-permute-start(bf16[8,528,128]{2,1,0:T(8,128)(2,1)} %get-tuple-element.57), channel_id=1, source_target_pairs={{0,24},{1,25},{2,26},{3,27},{4,28},{5,29},{6,30},{7,31},{8,0},{9,1... | collective-permute-start | bytes 3244040 | tf_op jit(solution)/shard_map/ppermute | solution.py:599
  121.0 50.8 %collective-permute-start = (bf16[8,528,128]{2,1,0:T(8,128)(2,1)}, bf16[8,528,128]{2,1,0:T(8,128)(2,1)S(1)}, u32[]{:S(2)}, u32[]{:S(2)}) collective-permute-start(bf16[8,528,128]{2,1,0:T(8,128)(2,1)} %get-tuple-element.55), channel_id=1, source_target_pairs={{0,8},{1,9},{2,10},{3,11},{4,12},{5,13},{6,14},{7,15},{8,16},{9,17... | collective-permute-start | bytes 3244040 | tf_op jit(solution)/shard_map/ppermute | solution.py:599
  123.2 48.6 %collective-permute-start.1 = (bf16[8,528,128]{2,1,0:T(8,128)(2,1)}, bf16[8,528,128]{2,1,0:T(8,128)(2,1)S(1)}, u32[]{:S(2)}, u32[]{:S(2)}) collective-permute-start(bf16[8,528,128]{2,1,0:T(8,128)(2,1)} %get-tuple-element.56), channel_id=1, source_target_pairs={{0,16},{1,17},{2,18},{3,19},{4,20},{5,21},{6,22},{7,23},{8,24},{9,... | collective-permute-start | bytes 3244040 | tf_op jit(solution)/shard_map/ppermute | solution.py:599
  125.6 20.4 %collective-permute-start.3 = (bf16[3,528,128]{2,1,0:T(8,128)(2,1)S(1)}, bf16[3,528,128]{2,1,0:T(8,128)(2,1)S(1)}, u32[]{:S(2)}, u32[]{:S(2)}) collective-permute-start(bf16[3,528,128]{2,1,0:T(8,128)(2,1)S(1)} %copy-done.6), channel_id=1, source_target_pairs={{0,1},{1,2},{2,3},{3,4},{4,5},{5,6},{6,7},{7,0},{8,9},{9,10},{10,1... | collective-permute-start | bytes 1216520 | tf_op jit(solution)/shard_map/ppermute | solution.py:594
  127.3 38.1 %collective-permute-start.4 = (bf16[3,528,128]{2,1,0:T(8,128)(2,1)S(1)}, bf16[3,528,128]{2,1,0:T(8,128)(2,1)S(1)}, u32[]{:S(2)}, u32[]{:S(2)}) collective-permute-start(bf16[3,528,128]{2,1,0:T(8,128)(2,1)S(1)} %copy-done.5), channel_id=1, source_target_pairs={{0,2},{1,3},{2,4},{3,5},{4,6},{5,7},{6,0},{7,1},{8,10},{9,11},{10,... | collective-permute-start | bytes 1216520 | tf_op jit(solution)/shard_map/ppermute | solution.py:594
  146.0 29.8 %copy-start.11 = (bf16[3,528,128]{2,1,0:T(8,128)(2,1)}, bf16[3,528,128]{2,1,0:T(8,128)(2,1)S(1)}, u32[]{:S(2)}) copy-start(bf16[3,528,128]{2,1,0:T(8,128)(2,1)S(1)} %collective-permute-done.3.rest_1_) | copy-start | bytes 1216516
  146.0 107.7 %collective-permute-start.5 = (bf16[3,528,128]{2,1,0:T(8,128)(2,1)S(1)}, bf16[3,528,128]{2,1,0:T(8,128)(2,1)S(1)}, u32[]{:S(2)}, u32[]{:S(2)}) collective-permute-start(bf16[3,528,128]{2,1,0:T(8,128)(2,1)S(1)} %copy-done.4), channel_id=1, source_target_pairs={{0,3},{1,4},{2,5},{3,6},{4,7},{5,0},{6,1},{7,2},{8,11},{9,12},{10,... | collective-permute-start | bytes 1216520 | tf_op jit(solution)/shard_map/ppermute | solution.py:594
  165.4 10.4 %copy-start.12 = (bf16[3,528,128]{2,1,0:T(8,128)(2,1)}, bf16[3,528,128]{2,1,0:T(8,128)(2,1)S(1)}, u32[]{:S(2)}) copy-start(bf16[3,528,128]{2,1,0:T(8,128)(2,1)S(1)} %collective-permute-done.4.rest_2_) | copy-start | bytes 1216516
  165.4 88.3 %collective-permute-start.6 = (bf16[3,528,128]{2,1,0:T(8,128)(2,1)S(1)}, bf16[3,528,128]{2,1,0:T(8,128)(2,1)}, u32[]{:S(2)}, u32[]{:S(2)}) collective-permute-start(bf16[3,528,128]{2,1,0:T(8,128)(2,1)S(1)} %copy-done.3), channel_id=1, source_target_pairs={{0,4},{1,5},{2,6},{3,7},{4,0},{5,1},{6,2},{7,3},{8,12},{9,13},{10,... | collective-permute-start | bytes 1216520 | tf_op jit(solution)/shard_map/ppermute | solution.py:594
  165.4 81.5 %copy-start.7 = (bf16[8,528,128]{2,1,0:T(8,128)(2,1)}, bf16[8,528,128]{2,1,0:T(8,128)(2,1)S(1)}, u32[]{:S(2)}) copy-start(bf16[8,528,128]{2,1,0:T(8,128)(2,1)S(1)} %collective-permute-done.2.b3) | copy-start | bytes 3244036
  165.4 88.2 %collective-permute-start.7 = (bf16[3,528,128]{2,1,0:T(8,128)(2,1)S(1)}, bf16[3,528,128]{2,1,0:T(8,128)(2,1)}, u32[]{:S(2)}, u32[]{:S(2)}) collective-permute-start(bf16[3,528,128]{2,1,0:T(8,128)(2,1)S(1)} %copy-done.2), channel_id=1, source_target_pairs={{0,5},{1,6},{2,7},{3,0},{4,1},{5,2},{6,3},{7,4},{8,13},{9,14},{10,... | collective-permute-start | bytes 1216520 | tf_op jit(solution)/shard_map/ppermute | solution.py:594
  171.8 4.0 %copy-start.8 = (bf16[8,528,128]{2,1,0:T(8,128)(2,1)}, bf16[8,528,128]{2,1,0:T(8,128)(2,1)S(1)}, u32[]{:S(2)}) copy-start(bf16[8,528,128]{2,1,0:T(8,128)(2,1)S(1)} %collective-permute-done.b1) | copy-start | bytes 3244036
  171.8 81.9 %collective-permute-start.8 = (bf16[3,528,128]{2,1,0:T(8,128)(2,1)S(1)}, bf16[3,528,128]{2,1,0:T(8,128)(2,1)}, u32[]{:S(2)}, u32[]{:S(2)}) collective-permute-start(bf16[3,528,128]{2,1,0:T(8,128)(2,1)S(1)} %copy-done.1), channel_id=1, source_target_pairs={{0,6},{1,7},{2,0},{3,1},{4,2},{5,3},{6,4},{7,5},{8,14},{9,15},{10,... | collective-permute-start | bytes 1216520 | tf_op jit(solution)/shard_map/ppermute | solution.py:594
  171.8 4.0 %copy-start.9 = (bf16[8,528,128]{2,1,0:T(8,128)(2,1)}, bf16[8,528,128]{2,1,0:T(8,128)(2,1)S(1)}, u32[]{:S(2)}) copy-start(bf16[8,528,128]{2,1,0:T(8,128)(2,1)S(1)} %collective-permute-done.1.b2) | copy-start | bytes 3244036
  171.8 81.9 %collective-permute-start.9 = (bf16[3,528,128]{2,1,0:T(8,128)(2,1)S(1)}, bf16[3,528,128]{2,1,0:T(8,128)(2,1)}, u32[]{:S(2)}, u32[]{:S(2)}) collective-permute-start(bf16[3,528,128]{2,1,0:T(8,128)(2,1)S(1)} %copy-done), channel_id=1, source_target_pairs={{0,7},{1,0},{2,1},{3,2},{4,3},{5,4},{6,5},{7,6},{8,15},{9,8},{10,9... | collective-permute-start | bytes 1216520 | tf_op jit(solution)/shard_map/ppermute | solution.py:594
  253.7 0.8 copy-start.13
  254.4 19.0 %copy-start.10 = (f32[1024,128]{1,0:T(8,128)S(1)}, f32[1024,128]{1,0:T(8,128)}, u32[]{:S(2)}) copy-start(f32[1024,128]{1,0:T(8,128)} %get-tuple-element.62) | copy-start | bytes 1572868

commit v5 on v4

--- a/solution.py
+++ b/solution.py
@@ -468,6 +468,18 @@
     end(c)
     s1[...] = ((b1[0] + b1[1]) + (b1[2] + b1[3])) + ((b1[4] + b1[5]) + (b1[6] + b1[7]))
     c = swap(1, NZ, at_z, lambda i: s1.at[rows(lax.rem(z + i, NZ), 16)], b2.at[z])
+    late = [
+        pltpu.make_async_remote_copy(
+            blk_ref.at[y * NZ + lax.rem(z + r, NZ)],
+            late_ref.at[m],
+            ls.at[m],
+            lr.at[m],
+            device_id=at_z(r),
+            device_id_type=MESH,
+        )
+        for m, r in enumerate(LATE)
+    ]
+    late[1].start()
     b2[z] = s1[rows(z, 16), :]
     end(c)
     s2[...] = ((b2[0] + b2[1]) + (b2[2] + b2[3])) + ((b2[4] + b2[5]) + (b2[6] + b2[7]))
@@ -476,19 +488,8 @@
     end(c)
     s3[...] = ((b3[0] + b3[1]) + (b3[2] + b3[3])) * scale
     c = swap(3, NZ, at_z, lambda i: s3, b4.at[rows(z, 16)])
-    late = [
-        pltpu.make_async_remote_copy(
-            blk_ref.at[y * NZ + lax.rem(z + r, NZ)],
-            late_ref.at[m],
-            ls.at[m],
-            lr.at[m],
-            device_id=at_z(r),
-            device_id_type=MESH,
-        )
-        for m, r in enumerate(LATE)
-    ]
-    for copy in late:
-        copy.start()
+    for m in (0, 2):
+        late[m].start()
     b4[rows(z, 16), :] = s3[...]
     end(c)
     c = swap(4, ND, at_dp, lambda i: b4, s4.at[rows(dp, 128)])

time: 279 us -> 283 us (1.014)
  Pallas kernels: 215 us -> 219 us
    pallas_call x1, Pallas kernels: 71.1 us -> 75.1 us  [total(): pl.pallas_call(lambda *refs: total_kernel(scale, *refs), out_shape=(jax.S...]
  transfers between devices with their start and end apart: 10 -> 10, of which waited for: 3 -> 3; matrix products, arithmetic and copies ran while one was open for 0% -> 0% of each run, Pallas kernels for 37% -> 38%
where the time goes in v5:
time: 283 us; the launch traced here: 278 us
  Pallas kernels  219 us (77%)
  waiting for transfers between devices  39.8 us (14%)
  starting transfers between devices  17.1 us (6%)
    pallas_call x1, Pallas kernels, total(): pl.pallas_call(lambda *refs: total_kernel(scale, *refs), out_shape=(jax.S...  75.1 us
    pallas_call x1, Pallas kernels, exchange(): pl.pallas_call(exchange_kernel, out_shape=(jax.ShapeDtypeStruct((NZ, PAR,...  64.4 us
    pallas_call x2, Pallas kernels, proxy(): pl.pallas_call(lambda *refs: proxy_kernel(distances, *refs), out_shape=(j...  47.5 us
    ppermute x7, waiting for transfers between devices, along_z(): lax.ppermute(v, 'space', [(d, d // NZ * NZ + (d + s) % NZ) for d in range...  36.9 us
    pallas_call x1, Pallas kernels, owner(): pl.pallas_call(owner_kernel, out_shape=jax.ShapeDtypeStruct((PAR, 128), B...  19 us
    ppermute x7, starting transfers between devices, along_z(): lax.ppermute(v, 'space', [(d, d // NZ * NZ + (d + s) % NZ) for d in range...  10.3 us
    ppermute x3, starting transfers between devices, along_y(): return lax.ppermute(v, 'space', [(d, (d + i * NZ) % NS) for d in range(NS)])  6.76 us
    pallas_call x1, Pallas kernels, unpack(): pl.pallas_call(unpack_kernel, out_shape=jax.ShapeDtypeStruct((rows, 128),...  6.7 us
  transfers between devices with their start and end apart: 10, of which 3 were waited for; matrix products, arithmetic and copies ran while one was open for 0% of the time, Pallas kernels for 38%

profile of v5, /device:TPU:2, one launch (start us, length us, event | category | flops | bytes accessed | tf_op | source)
XLA Modules:
  0.0 278.2 jit_solution(7048255249072814963)
XLA Ops:
  0.6 6.2 %pack.1 = (bf16[32,528,128]{2,1,0:T(8,128)(2,1)}, s32[32,8,128]{2,1,0:T(8,128)}, s32[32,8,128]{2,1,0:T(8,128)}, s32[32]{0:T(128)}, s32[32]{0:T(128)}, /*index=5*/s32[32]{0:T(128)}) custom-call(s32[64,128]{1,0:T(8,128)} %bitcast.22, s32[64,128]{1,0:T(8,128)} %bitcast.23, bf16[8192,128]{1,0:T(8,128)(2,1)} %bitcast.16), custom_call_target="tpu_custom_call" | custom-call | bytes 28800000 | tf_op jit(solution)/shard_map/pack/pallas_call | solution.py:84
  6.8 64.4 %exchange.1 = (bf16[8,2048,128]{2,1,0:T(8,128)(2,1)}, s32[32,8,128]{2,1,0:T(8,128)}, s32[32,8,128]{2,1,0:T(8,128)}, bf16[8,528,128]{2,1,0:T(8,128)(2,1)}, bf16[3...) custom-call(bf16[2048,128]{1,0:T(8,128)(2,1)} %bitcast.18, ...), custom_call_target="tpu_custom_call" | custom-call | bytes 180000000 | tf_op jit(solution)/shard_map/exchange/pallas_call | solution.py:233
  71.3 23.8 %proxy.3 = (bf16[8,528,128]{2,1,0:T(8,128)(2,1)}, bf16[8,528,128]{2,1,0:T(8,128)(2,1)}, f32[1024,128]{1,0:T(8,128)}) custom-call(s32[32768]{0:T(1024)} %bitcast.14, s32[32,8,128]{2,1,0:T(8,128)} %get-tuple-element.38.refs_1_, bf16[16384,128]{1,0:T(8,128)(2,1)} %bitcast.11, bf16[8,128,128]{2,1,0:T(8,128)(2,1)} %refs_3_.3, ...), custom_call_target="tpu_custom_call" | custom-call | bytes 72000000 | tf_op jit(solution)/shard_map/proxy/pallas_call | solution.py:335
  95.2 2.2 collective-permute-start.2
  97.4 23.6 %proxy.2 = (bf16[8,528,128]{2,1,0:T(8,128)(2,1)}, bf16[8,528,128]{2,1,0:T(8,128)(2,1)}, f32[1024,128]{1,0:T(8,128)}) custom-call(s32[32768]{0:T(1024)} %bitcast.15, s32[32,8,128]{2,1,0:T(8,128)} %get-tuple-element.38.refs_1_, bf16[16384,128]{1,0:T(8,128)(2,1)} %bitcast.12, bf16[8,128,128]{2,1,0:T(8,128)(2,1)} %refs_3_.3, ...), custom_call_target="tpu_custom_call" | custom-call | bytes 72000000 | tf_op jit(solution)/shard_map/proxy/pallas_call | solution.py:335
  121.0 2.2 collective-permute-start
  123.2 2.3 collective-permute-start.1
  125.6 1.7 collective-permute-start.3
  127.3 1.2 collective-permute-start.4
  128.5 17.5 %collective-permute-done.3.rest_1_ = bf16[3,528,128]{2,1,0:T(8,128)(2,1)S(1)} collective-permute-done((bf16[3,528,128]{2,1,0:T(8,128)(2,1)S(1)}, bf16[3,528,128]{2,1,0:T(8,128)(2,1)S(1)}, u32[]{:S(2)}, u32[]{:S(2)}) %collective-permute-start.3) | collective-permute-done | bytes 405536 | tf_op jit(solution)/shard_map/ppermute | solution.py:595
  146.0 19.4 %collective-permute-done.4.rest_2_ = bf16[3,528,128]{2,1,0:T(8,128)(2,1)S(1)} collective-permute-done((bf16[3,528,128]{2,1,0:T(8,128)(2,1)S(1)}, bf16[3,528,128]{2,1,0:T(8,128)(2,1)S(1)}, u32[]{:S(2)}, u32[]{:S(2)}) %collective-permute-start.4) | collective-permute-done | bytes 405536 | tf_op jit(solution)/shard_map/ppermute | solution.py:595
  165.4 0.0 collective-permute-done.2.b3
  165.4 3.4 %collective-permute-start.7 = (bf16[3,528,128]{2,1,0:T(8,128)(2,1)S(1)}, bf16[3,528,128]{2,1,0:T(8,128)(2,1)}, u32[]{:S(2)}, u32[]{:S(2)}) collective-permute-start(bf16[3,528,128]{2,1,0:T(8,128)(2,1)S(1)} %copy-done.2), channel_id=1, source_target_pairs={{0,5},{1,6},{2,7},{3,0},{4,1},{5,2},{6,3},{7,4},{8,13},{9,14},{10,... | collective-permute-start | bytes 1216520 | tf_op jit(solution)/shard_map/ppermute | solution.py:595
  168.8 3.0 %collective-permute-done.b1 = bf16[8,528,128]{2,1,0:T(8,128)(2,1)S(1)} collective-permute-done((bf16[8,528,128]{2,1,0:T(8,128)(2,1)}, bf16[8,528,128]{2,1,0:T(8,128)(2,1)S(1)}, u32[]{:S(2)}, u32[]{:S(2)}) %collective-permute-start) | collective-permute-done | bytes 1081376 | tf_op jit(solution)/shard_map/ppermute | solution.py:600
  171.8 0.0 collective-permute-done.1.b2
  171.8 4.0 %collective-permute-start.9 = (bf16[3,528,128]{2,1,0:T(8,128)(2,1)S(1)}, bf16[3,528,128]{2,1,0:T(8,128)(2,1)}, u32[]{:S(2)}, u32[]{:S(2)}) collective-permute-start(bf16[3,528,128]{2,1,0:T(8,128)(2,1)S(1)} %copy-done), channel_id=1, source_target_pairs={{0,7},{1,0},{2,1},{3,2},{4,3},{5,4},{6,5},{7,6},{8,15},{9,8},{10,9... | collective-permute-start | bytes 1216520 | tf_op jit(solution)/shard_map/ppermute | solution.py:595
  175.8 75.1 %total.1 = (f32[1024,128]{1,0:T(8,128)}, bf16[3,528,128]{2,1,0:T(8,128)(2,1)}) custom-call(f32[1024,128]{1,0:T(8,128)} %get-tuple-element.48.refs_0_, f32[1024,128]{1,0:T(8,128)} %get-tuple-element.49.refs_1_, bf16[32,528,128]{2,1,0:T(8,128)(2,1)} %get-tuple-element.35.blk_ref.refs_4_.refs_2_), custom_call_target="tpu_custom_call" | custom-call | bytes 118800000 | tf_op jit(solution)/shard_map/total/pallas_call | solution.py:504
  250.9 6.7 %unpack.1 = bf16[8192,128]{1,0:T(8,128)(2,1)} custom-call(s32[32]{0:T(128)} %get-tuple-element.51.first_ref, s32[32]{0:T(128)} %get-tuple-element.52.lo_ref, s32[32]{0:T(128)} %get-tuple-element.53.hi_ref, bf16[8,528,128]{2,1,0:T(8,128)(2,1)} %get-tuple-element.54.b0, bf16[8,528,128]{2,1,0:T(8,128)(2,1)} %copy-done.8, bf16[8,528,128]{2,1,0:T(8,128)(2,1)} %copy-done.9, ...), custom_call_target="tpu_custom_call" | custom-call | bytes 28800000 | tf_op jit(solution)/shard_map/unpack/pallas_call | solution.py:574
  257.6 0.0 collective-permute-done.5.rest_3_
  257.6 0.0 collective-permute-done.6.rest_4_
  257.7 0.0 collective-permute-done.9.rest_7_
  257.7 0.7 copy-done.13
  258.4 19.0 %owner.1 = bf16[2048,128]{1,0:T(8,128)(2,1)} custom-call(s32[32768]{0:T(1024)} %bitcast.21, bf16[1024,128]{1,0:T(8,128)(2,1)} %bitcast.13, bf16[32,528,128]{2,1,0:T(8,128)(2,1)} %get-tuple-element.35.blk_ref.refs_4_.refs_2_, bf16[8,528,128]{2,1,0:T(8,128)(2,1)} %get-tuple-element.59.near_ref, bf16[3,528,128]{2,1,0:T(8,128)(2,1)} %get-tuple-element.60.late_ref, ...), custom_call_target="tpu_custom_call" | custom-call | bytes 64800000 | tf_op jit(solution)/shard_map/owner/pallas_call | solution.py:416
  277.4 0.8 copy.9
  (32 shorter events, 0.1 us)
Async XLA Ops:
  95.1 30.5 %copy-start.6 = (bf16[3,528,128]{2,1,0:T(8,128)(2,1)S(1)}, bf16[3,528,128]{2,1,0:T(8,128)(2,1)}, u32[]{:S(2)}) copy-start(bf16[3,528,128]{2,1,0:T(8,128)(2,1)} %get-tuple-element.41.refs_6_) | copy-start | bytes 1216516
  95.1 32.2 %copy-start.5 = (bf16[3,528,128]{2,1,0:T(8,128)(2,1)S(1)}, bf16[3,528,128]{2,1,0:T(8,128)(2,1)}, u32[]{:S(2)}) copy-start(bf16[3,528,128]{2,1,0:T(8,128)(2,1)} %get-tuple-element.42.refs_7_) | copy-start | bytes 1216516
  95.1 50.8 %copy-start.4 = (bf16[3,528,128]{2,1,0:T(8,128)(2,1)S(1)}, bf16[3,528,128]{2,1,0:T(8,128)(2,1)}, u32[]{:S(2)}) copy-start(bf16[3,528,128]{2,1,0:T(8,128)(2,1)} %get-tuple-element.43.refs_8_) | copy-start | bytes 1216516
  95.1 70.2 %copy-start.3 = (bf16[3,528,128]{2,1,0:T(8,128)(2,1)S(1)}, bf16[3,528,128]{2,1,0:T(8,128)(2,1)}, u32[]{:S(2)}) copy-start(bf16[3,528,128]{2,1,0:T(8,128)(2,1)} %get-tuple-element.44.refs_9_) | copy-start | bytes 1216516
  95.1 70.3 %copy-start.2 = (bf16[3,528,128]{2,1,0:T(8,128)(2,1)S(1)}, bf16[3,528,128]{2,1,0:T(8,128)(2,1)}, u32[]{:S(2)}) copy-start(bf16[3,528,128]{2,1,0:T(8,128)(2,1)} %get-tuple-element.45.refs_10_) | copy-start | bytes 1216516
  95.2 76.6 %copy-start.1 = (bf16[3,528,128]{2,1,0:T(8,128)(2,1)S(1)}, bf16[3,528,128]{2,1,0:T(8,128)(2,1)}, u32[]{:S(2)}) copy-start(bf16[3,528,128]{2,1,0:T(8,128)(2,1)} %get-tuple-element.46.refs_11_) | copy-start | bytes 1216516
  95.2 76.7 %copy-start = (bf16[3,528,128]{2,1,0:T(8,128)(2,1)S(1)}, bf16[3,528,128]{2,1,0:T(8,128)(2,1)}, u32[]{:S(2)}) copy-start(bf16[3,528,128]{2,1,0:T(8,128)(2,1)} %get-tuple-element.47.refs_12_) | copy-start | bytes 1216516
  95.2 70.2 %collective-permute-start.2 = (bf16[8,528,128]{2,1,0:T(8,128)(2,1)}, bf16[8,528,128]{2,1,0:T(8,128)(2,1)S(1)}, u32[]{:S(2)}, u32[]{:S(2)}) collective-permute-start(bf16[8,528,128]{2,1,0:T(8,128)(2,1)} %get-tuple-element.57), channel_id=1, source_target_pairs={{0,24},{1,25},{2,26},{3,27},{4,28},{5,29},{6,30},{7,31},{8,0},{9,1... | collective-permute-start | bytes 3244040 | tf_op jit(solution)/shard_map/ppermute | solution.py:600
  121.0 50.8 %collective-permute-start = (bf16[8,528,128]{2,1,0:T(8,128)(2,1)}, bf16[8,528,128]{2,1,0:T(8,128)(2,1)S(1)}, u32[]{:S(2)}, u32[]{:S(2)}) collective-permute-start(bf16[8,528,128]{2,1,0:T(8,128)(2,1)} %get-tuple-element.55), channel_id=1, source_target_pairs={{0,8},{1,9},{2,10},{3,11},{4,12},{5,13},{6,14},{7,15},{8,16},{9,17... | collective-permute-start | bytes 3244040 | tf_op jit(solution)/shard_map/ppermute | solution.py:600
  123.2 48.6 %collective-permute-start.1 = (bf16[8,528,128]{2,1,0:T(8,128)(2,1)}, bf16[8,528,128]{2,1,0:T(8,128)(2,1)S(1)}, u32[]{:S(2)}, u32[]{:S(2)}) collective-permute-start(bf16[8,528,128]{2,1,0:T(8,128)(2,1)} %get-tuple-element.56), channel_id=1, source_target_pairs={{0,16},{1,17},{2,18},{3,19},{4,20},{5,21},{6,22},{7,23},{8,24},{9,... | collective-permute-start | bytes 3244040 | tf_op jit(solution)/shard_map/ppermute | solution.py:600
  125.6 20.4 %collective-permute-start.3 = (bf16[3,528,128]{2,1,0:T(8,128)(2,1)S(1)}, bf16[3,528,128]{2,1,0:T(8,128)(2,1)S(1)}, u32[]{:S(2)}, u32[]{:S(2)}) collective-permute-start(bf16[3,528,128]{2,1,0:T(8,128)(2,1)S(1)} %copy-done.6), channel_id=1, source_target_pairs={{0,1},{1,2},{2,3},{3,4},{4,5},{5,6},{6,7},{7,0},{8,9},{9,10},{10,1... | collective-permute-start | bytes 1216520 | tf_op jit(solution)/shard_map/ppermute | solution.py:595
  127.3 38.1 %collective-permute-start.4 = (bf16[3,528,128]{2,1,0:T(8,128)(2,1)S(1)}, bf16[3,528,128]{2,1,0:T(8,128)(2,1)S(1)}, u32[]{:S(2)}, u32[]{:S(2)}) collective-permute-start(bf16[3,528,128]{2,1,0:T(8,128)(2,1)S(1)} %copy-done.5), channel_id=1, source_target_pairs={{0,2},{1,3},{2,4},{3,5},{4,6},{5,7},{6,0},{7,1},{8,10},{9,11},{10,... | collective-permute-start | bytes 1216520 | tf_op jit(solution)/shard_map/ppermute | solution.py:595
  146.0 29.8 %copy-start.11 = (bf16[3,528,128]{2,1,0:T(8,128)(2,1)}, bf16[3,528,128]{2,1,0:T(8,128)(2,1)S(1)}, u32[]{:S(2)}) copy-start(bf16[3,528,128]{2,1,0:T(8,128)(2,1)S(1)} %collective-permute-done.3.rest_1_) | copy-start | bytes 1216516
  146.0 111.7 %collective-permute-start.5 = (bf16[3,528,128]{2,1,0:T(8,128)(2,1)S(1)}, bf16[3,528,128]{2,1,0:T(8,128)(2,1)S(1)}, u32[]{:S(2)}, u32[]{:S(2)}) collective-permute-start(bf16[3,528,128]{2,1,0:T(8,128)(2,1)S(1)} %copy-done.4), channel_id=1, source_target_pairs={{0,3},{1,4},{2,5},{3,6},{4,7},{5,0},{6,1},{7,2},{8,11},{9,12},{10,... | collective-permute-start | bytes 1216520 | tf_op jit(solution)/shard_map/ppermute | solution.py:595
  165.4 10.4 %copy-start.12 = (bf16[3,528,128]{2,1,0:T(8,128)(2,1)}, bf16[3,528,128]{2,1,0:T(8,128)(2,1)S(1)}, u32[]{:S(2)}) copy-start(bf16[3,528,128]{2,1,0:T(8,128)(2,1)S(1)} %collective-permute-done.4.rest_2_) | copy-start | bytes 1216516
  165.4 92.2 %collective-permute-start.6 = (bf16[3,528,128]{2,1,0:T(8,128)(2,1)S(1)}, bf16[3,528,128]{2,1,0:T(8,128)(2,1)}, u32[]{:S(2)}, u32[]{:S(2)}) collective-permute-start(bf16[3,528,128]{2,1,0:T(8,128)(2,1)S(1)} %copy-done.3), channel_id=1, source_target_pairs={{0,4},{1,5},{2,6},{3,7},{4,0},{5,1},{6,2},{7,3},{8,12},{9,13},{10,... | collective-permute-start | bytes 1216520 | tf_op jit(solution)/shard_map/ppermute | solution.py:595
  165.4 85.5 %copy-start.7 = (bf16[8,528,128]{2,1,0:T(8,128)(2,1)}, bf16[8,528,128]{2,1,0:T(8,128)(2,1)S(1)}, u32[]{:S(2)}) copy-start(bf16[8,528,128]{2,1,0:T(8,128)(2,1)S(1)} %collective-permute-done.2.b3) | copy-start | bytes 3244036
  165.4 92.2 %collective-permute-start.7 = (bf16[3,528,128]{2,1,0:T(8,128)(2,1)S(1)}, bf16[3,528,128]{2,1,0:T(8,128)(2,1)}, u32[]{:S(2)}, u32[]{:S(2)}) collective-permute-start(bf16[3,528,128]{2,1,0:T(8,128)(2,1)S(1)} %copy-done.2), channel_id=1, source_target_pairs={{0,5},{1,6},{2,7},{3,0},{4,1},{5,2},{6,3},{7,4},{8,13},{9,14},{10,... | collective-permute-start | bytes 1216520 | tf_op jit(solution)/shard_map/ppermute | solution.py:595
  171.8 4.0 %copy-start.8 = (bf16[8,528,128]{2,1,0:T(8,128)(2,1)}, bf16[8,528,128]{2,1,0:T(8,128)(2,1)S(1)}, u32[]{:S(2)}) copy-start(bf16[8,528,128]{2,1,0:T(8,128)(2,1)S(1)} %collective-permute-done.b1) | copy-start | bytes 3244036
  171.8 85.8 %collective-permute-start.8 = (bf16[3,528,128]{2,1,0:T(8,128)(2,1)S(1)}, bf16[3,528,128]{2,1,0:T(8,128)(2,1)}, u32[]{:S(2)}, u32[]{:S(2)}) collective-permute-start(bf16[3,528,128]{2,1,0:T(8,128)(2,1)S(1)} %copy-done.1), channel_id=1, source_target_pairs={{0,6},{1,7},{2,0},{3,1},{4,2},{5,3},{6,4},{7,5},{8,14},{9,15},{10,... | collective-permute-start | bytes 1216520 | tf_op jit(solution)/shard_map/ppermute | solution.py:595
  171.8 4.0 %copy-start.9 = (bf16[8,528,128]{2,1,0:T(8,128)(2,1)}, bf16[8,528,128]{2,1,0:T(8,128)(2,1)S(1)}, u32[]{:S(2)}) copy-start(bf16[8,528,128]{2,1,0:T(8,128)(2,1)S(1)} %collective-permute-done.1.b2) | copy-start | bytes 3244036
  171.8 85.8 %collective-permute-start.9 = (bf16[3,528,128]{2,1,0:T(8,128)(2,1)S(1)}, bf16[3,528,128]{2,1,0:T(8,128)(2,1)}, u32[]{:S(2)}, u32[]{:S(2)}) collective-permute-start(bf16[3,528,128]{2,1,0:T(8,128)(2,1)S(1)} %copy-done), channel_id=1, source_target_pairs={{0,7},{1,0},{2,1},{3,2},{4,3},{5,4},{6,5},{7,6},{8,15},{9,8},{10,9... | collective-permute-start | bytes 1216520 | tf_op jit(solution)/shard_map/ppermute | solution.py:595
  257.6 0.8 copy-start.13
  258.4 19.0 %copy-start.10 = (f32[1024,128]{1,0:T(8,128)S(1)}, f32[1024,128]{1,0:T(8,128)}, u32[]{:S(2)}) copy-start(f32[1024,128]{1,0:T(8,128)} %get-tuple-element.62) | copy-start | bytes 1572868
